TPU v7x, 512 devices: a whole 4x8x8 slice. The times are simulated.
512 devices in a mesh: segment: 4 (over x), row: 8 (over z), col: 16 (over y, core).
Axes of the slice: x: 4, y: 8, z: 8, core: 2. Of those that a mesh axis runs over, the one named last changes fastest.
Arguments:
- saved_inputs: bfloat16 [4, 1, 128, 256, 256], P('segment', None, 'row', 'col'), may hold values from -6 to 6
- out_grad: bfloat16 [1, 128, 256, 256], P(None, 'row', 'col'), may hold values from -6 to 6
- tissue: int32 [1, 8, 16], P(None, 'row', 'col'), may hold values 0 or 1
- conv_taps: float32 [4, 7, 7, 256], P('segment'), may hold values from -0.875 to 0.875
- conv_bias: float32 [4, 256], P('segment'), may hold values from -3 to 3
- norm_gain: float32 [4, 256], P('segment'), may hold values from 0.1 to 1.9
- norm_bias: float32 [4, 256], P('segment'), may hold values from -3 to 3
- w_in: bfloat16 [4, 256, 1024], P('segment'), may hold values from -0.375 to 0.375
- b_in: float32 [4, 1024], P('segment'), may hold values from -3 to 3
- w_out: bfloat16 [4, 1024, 256], P('segment'), may hold values from -0.1875 to 0.1875
- layer_scale: float32 [4, 256], P('segment'), may hold values from 0.3 to 1.5
Outputs:
- section_grads: bfloat16 [4, 1, 128, 256, 256], P('segment', None, 'row', 'col')
- grad_w_in: float32 [4, 256, 1024], P('segment', 'col')
- grad_w_out: float32 [4, 1024, 256], P('segment', 'col')
- grad_taps: float32 [4, 7, 7, 256], P('segment')
Inputs may be any that keep to these rules, and one draw needn't show every extreme that they name: 1 marks a tile that holds tissue, 0 an empty one.
All inputs are finite; a program needn't handle non-finite values. No bound on the sum of `tissue` on one device may be relied on, other than what follows from the above.
Results may differ from a plain program's by a relative error of at most 0.013.
Values may be sent and summed in bfloat16 or wider, within the bound.
A program may use at most 128 MiB of HBM per device.

v0:
```python
import math

import jax
import jax.numpy as jnp
from jax import lax
from jax.sharding import PartitionSpec as P

epsilon = 1e-06


def with_halo(block, sides, width):
    for axis, dim in sides:
        count = lax.axis_size(axis)
        forward = [(i, i + 1) for i in range(count - 1)]
        backward = [(target, source) for source, target in forward]
        low = lax.ppermute(
            lax.slice_in_dim(block, block.shape[dim] - width, None, axis=dim), axis, forward
        )
        high = lax.ppermute(lax.slice_in_dim(block, 0, width, axis=dim), axis, backward)
        block = jnp.concatenate([low, block, high], axis=dim)
    return block


def shifted(block, axis, distance):
    devices = range(lax.axis_size(axis))
    route = [(i - distance, i) for i in devices if i - distance in devices]
    return lax.ppermute(block, axis, route)


def depthwise(padded, conv_taps, height, across):
    side = conv_taps.shape[0]
    total = jnp.zeros((height, across, padded.shape[-1]), jnp.float32)
    for shift_r in range(side):
        for shift_c in range(side):
            total = total + conv_taps[shift_r, shift_c] * padded[
                shift_r : shift_r + height, shift_c : shift_c + across
            ].astype(jnp.float32)
    return total


def transposed(padded_grad, conv_taps, height, across):
    side = conv_taps.shape[0]
    margin = side // 2
    total = jnp.zeros((height, across, padded_grad.shape[-1]), jnp.float32)
    for shift_r in range(side):
        for shift_c in range(side):
            start_r = 2 * margin - shift_r
            start_c = 2 * margin - shift_c
            total = total + conv_taps[shift_r, shift_c] * padded_grad[
                start_r : start_r + height, start_c : start_c + across
            ].astype(jnp.float32)
    return total


def kernel_grad(padded, grad, side, height, across):
    grad_wide = grad.astype(jnp.float32)
    pieces = []
    for shift_r in range(side):
        for shift_c in range(side):
            window = padded[shift_r : shift_r + height, shift_c : shift_c + across].astype(
                jnp.float32
            )
            pieces.append(jnp.sum(window * grad_wide, axis=(0, 1)))
    return jnp.stack(pieces).reshape(side, side, -1)


def normalize(conv_out, norm_gain, norm_bias):
    average = jnp.mean(conv_out, axis=-1, keepdims=True)
    centred = conv_out - average
    spread = jnp.mean(centred * centred, axis=-1, keepdims=True)
    inv_std = lax.rsqrt(spread + epsilon)
    standard = centred * inv_std
    normed = (standard * norm_gain + norm_bias).astype(jnp.bfloat16)
    return (standard, inv_std, normed)


def mlp_back(normed, branch_grad, norm_gain, w_in, b_in, w_out):
    pre_gate = jnp.dot(normed, w_in, preferred_element_type=jnp.float32) + b_in
    gated, gelu_back = jax.vjp(jax.nn.gelu, pre_gate)
    hidden = gated.astype(jnp.bfloat16)
    grad_out = jnp.dot(hidden.T, branch_grad, preferred_element_type=jnp.float32)
    hidden_grad = jnp.dot(branch_grad, w_out.T, preferred_element_type=jnp.float32)
    pre_grad = gelu_back(hidden_grad)[0].astype(jnp.bfloat16)
    grad_in = jnp.dot(normed.T, pre_grad, preferred_element_type=jnp.float32)
    norm_grad = jnp.dot(pre_grad, w_in.T, preferred_element_type=jnp.float32) * norm_gain
    return (norm_grad, grad_in, grad_out)


def finish_norm(norm_grad, standard, inv_std):
    conv_grad = inv_std * (
        norm_grad
        - jnp.mean(norm_grad, axis=-1, keepdims=True)
        - standard * jnp.mean(norm_grad * standard, axis=-1, keepdims=True)
    )
    return conv_grad.astype(jnp.bfloat16)


def pixel_grad(conv_out, upstream, gate, norm_gain, norm_bias, w_in, b_in, w_out, layer_scale):
    standard, inv_std, normed = normalize(conv_out, norm_gain, norm_bias)
    branch_grad = (gate * layer_scale * upstream.astype(jnp.float32)).astype(jnp.bfloat16)
    norm_grad, grad_in, grad_out = mlp_back(normed, branch_grad, norm_gain, w_in, b_in, w_out)
    return (finish_norm(norm_grad, standard, inv_std), grad_in, grad_out)


def per_device(
    saved_inputs,
    out_grad,
    tissue,
    conv_taps,
    conv_bias,
    norm_gain,
    norm_bias,
    w_in,
    b_in,
    w_out,
    layer_scale,
):
    segments = lax.axis_size("segment")
    section = lax.axis_index("segment")
    col_count = lax.axis_size("col")
    crop_count, height, across, channels = out_grad.shape
    tiles_r = tissue.shape[1]
    tiles_c = tissue.shape[2]
    tile_side = height // tiles_r
    hidden_units = w_in.shape[2]
    taps = conv_taps[0]
    side = taps.shape[0]
    margin = side // 2
    bias_conv = conv_bias[0]
    gain_norm = norm_gain[0]
    bias_norm = norm_bias[0]
    weight_in = w_in[0]
    bias_in = b_in[0]
    weight_out = w_out[0]
    scale_layer = layer_scale[0]
    pixel_total = crop_count * height * across * lax.axis_size("row") * col_count
    norm_scale = 1.0 / math.sqrt(pixel_total)
    saved_pad = with_halo(saved_inputs[0], (("row", 1), ("col", 2)), margin)

    def zero_grads(pixels):
        return (
            jnp.zeros((pixels, channels), jnp.bfloat16),
            jnp.zeros((channels, hidden_units), jnp.float32),
            jnp.zeros((hidden_units, channels), jnp.float32),
        )

    def advance(step_index, loop_state):
        incoming, collected, sum_in, sum_out, sum_taps = loop_state
        crop_index = step_index - (segments - 1 - section)
        active = jnp.logical_and(crop_index >= 0, crop_index < crop_count)
        crop_index = jnp.clip(crop_index, 0, crop_count - 1)
        own_grad = lax.dynamic_index_in_dim(out_grad, crop_index, 0, keepdims=False)
        upstream = jnp.where(section == segments - 1, own_grad, incoming)
        saved_tile = lax.dynamic_index_in_dim(saved_pad, crop_index, 0, keepdims=False)
        conv_out = depthwise(saved_tile, taps, height, across) + bias_conv
        tile_marks = lax.dynamic_index_in_dim(tissue, crop_index, 0, keepdims=False)
        pixel_mask = jnp.broadcast_to(
            tile_marks.astype(jnp.float32)[:, None, :, None],
            (tiles_r, tile_side, tiles_c, tile_side),
        ).reshape(height * across, 1)

        def worked():
            return pixel_grad(
                conv_out.reshape(-1, channels),
                upstream.reshape(-1, channels),
                pixel_mask,
                gain_norm,
                bias_norm,
                weight_in,
                bias_in,
                weight_out,
                scale_layer,
            )

        def skipped():
            return zero_grads(height * across)

        grad_rows, add_in, add_out = lax.cond(active, worked, skipped)
        conv_grad = grad_rows.reshape(height, across, channels)
        sum_in = sum_in + add_in
        sum_out = sum_out + add_out
        sum_taps = sum_taps + kernel_grad(saved_tile, conv_grad, side, height, across)
        padded_grad = with_halo(conv_grad, (("row", 0), ("col", 1)), margin)
        input_grad = (
            upstream.astype(jnp.float32) + transposed(padded_grad, taps, height, across)
        ).astype(jnp.bfloat16)
        updated = lax.dynamic_update_index_in_dim(collected, input_grad, crop_index, 0)
        collected = jnp.where(active, updated, collected)
        passed = shifted(input_grad, "segment", -1)
        return (passed, collected, sum_in, sum_out, sum_taps)

    initial = (
        jnp.zeros((height, across, channels), jnp.bfloat16),
        jnp.zeros((crop_count, height, across, channels), jnp.bfloat16),
        jnp.zeros((channels, hidden_units), jnp.float32),
        jnp.zeros((hidden_units, channels), jnp.float32),
        jnp.zeros((side, side, channels), jnp.float32),
    )
    final_state = lax.fori_loop(0, crop_count + segments - 1, advance, initial)
    collected = final_state[1]
    sum_in = final_state[2]
    sum_out = final_state[3]
    sum_taps = final_state[4]
    summed_in, summed_out, summed_taps = lax.psum((sum_in, sum_out, sum_taps), ("row", "col"))
    column = lax.axis_index("col")
    share_in = lax.dynamic_slice_in_dim(
        summed_in, column * (channels // col_count), channels // col_count, 0
    )
    share_out = lax.dynamic_slice_in_dim(
        summed_out, column * (hidden_units // col_count), hidden_units // col_count, 0
    )
    return (
        collected[None],
        (share_in * norm_scale)[None],
        (share_out * norm_scale)[None],
        (summed_taps * norm_scale)[None],
    )


def solution(mesh):
    return jax.shard_map(
        per_device,
        mesh=mesh,
        in_specs=(
            P("segment", None, "row", "col", None),
            P(None, "row", "col", None),
            P(None, "row", "col"),
            P("segment", None, None, None),
            P("segment", None),
            P("segment", None),
            P("segment", None),
            P("segment", None, None),
            P("segment", None),
            P("segment", None, None),
            P("segment", None),
        ),
        out_specs=(
            P("segment", None, "row", "col", None),
            P("segment", "col", None),
            P("segment", "col", None),
            P("segment", None, None, None),
        ),
        check_vma=False,
    )
```

profile of v0, /device:TPU:1, one launch (start us, length us, event | category | flops | bytes accessed | tf_op | source)
XLA Modules:
  0.0 941.0 jit_solution(11491032198375591232)
XLA Ops:
  8.0 4.8 collective-permute-start.5
  14.1 3.9 collective-permute-done.6
  18.9 5.0 collective-permute-start.7
  30.4 409.2 %while.24 = (s32[]{:T(128)}, bf16[16,16,256]{2,1,0:T(8,128)(2,1)S(1)}, bf16[1,16,16,256]{3,2,1,0:T(8,128)(2,1)}, f32[256,1024]{1,0:T(8,128)S(1)}, f32[1024,256]{...) while((s32[]{:T(128)}, ...), condition=%wide.region_56.57_spmd.clone, body=%wide.region_0.56_spmd.clone.sunk | while | flops 713714432 | bytes 106633936 | solution.py:199
  30.4 2.2 slice_convert_fusion.53
  32.7 2.3 slice_convert_fusion.54
  86.2 5.2 collective-permute-start.1
  98.4 3.6 collective-permute-start.3
  105.5 3.1 bitcast_select_fusion.3
  110.1 5.0 collective-permute-done.4
  115.8 2.2 slice_convert_fusion.53
  118.0 2.3 slice_convert_fusion.54
  171.5 5.8 collective-permute-start.1
  179.8 2.5 select_add_fusion.7
  185.7 4.6 collective-permute-start.3
  193.8 3.1 bitcast_select_fusion.3
  198.4 4.3 collective-permute-done.4
  205.7 2.3 slice_convert_fusion.54
  259.2 5.5 collective-permute-start.1
  267.2 2.5 select_add_fusion.7
  272.9 5.5 collective-permute-start.3
  281.8 3.1 bitcast_select_fusion.3
  286.4 49.3 %collective-permute-done.4 = bf16[16,16,256]{2,1,0:T(8,128)(2,1)S(1)} collective-permute-done((bf16[16,16,256]{2,1,0:T(8,128)(2,1)S(1)}, bf16[16,16,256]{2,1,0:T(8,128)(2,1)S(1)}, u32[]{:S(2)}, u32[]{:S(2)}) %collective-permute-start.4) | collective-permute-done | bytes 131104 | tf_op jit(solution)/shard_map/while/body/eval_jaxpr/ppermute | solution.py:27
  338.6 2.3 slice_convert_fusion.54
  387.6 16.4 %conditional.3 = (bf16[256,256]{0,1:T(8,128)(2,1)}, f32[256,1024]{1,0:T(8,128)S(1)}, f32[1024,256]{1,0:T(8,128)S(1)}) conditional(s32[]{:T(128)} %convert_element_type.1669, () %tuple.232, (f32[16,16,256]{2,1,0:T(8,128)}, f32[16,16,256]{2,1,0:T(8,128)}, f32[256]{0:T(256)}, f32[16,16,256]{2,1,0:T(8,128)}, f32[16,16,256]{2,1,0:T(8,128)}, ...), branch_computations={%region_1.1_spmd, %region_2.6_spmd} | conditional | flops 687342080 | bytes 42378324 | solution.py:178
  387.6 9.6 %fusion.97 = (f32[16,16]{1,0:T(8,128)S(1)}, f32[16,16,256]{2,1,0:T(8,128)S(1)}) fusion(f32[256]{0:T(256)} %bitcast, f32[16,16,256]{2,1,0:T(8,128)} %get-tuple-element.800, f32[16,16,256]{2,1,0:T(8,128)} %get-tuple-element.801, f32[16,16,256]{2,1,0:T(8,128)} %get-tuple-element.798, f32[16,16,256]{2,1,0:T(8,128)} %get-tuple-element.799, ...), kind=kLoop, calls=%fused_computation.242 | loop fusion | flops 6487808 | bytes 25693184 | tf_op jit(solution)/shard_map/while/body/eval_jaxpr/cond/branch_1_fun/reduce_sum | solution.py:68
  407.6 5.2 collective-permute-start.1
  415.3 2.5 select_add_fusion.7
  421.1 5.4 collective-permute-start.3
  429.9 3.1 bitcast_select_fusion.3
  434.6 4.3 collective-permute-done.4
  440.6 490.0 %psum.23 = f32[7,7,256]{2,1,0:T(8,128)S(1)} all-reduce(f32[7,7,256]{2,1,0:T(8,128)S(1)} %copy-done.17), channel_id=1, replica_groups=mesh['segment'=4,'row'=8,'col'=16] {'row','col'}, use_global_device_ids=true, to_apply=%region_59.60 | all-reduce | flops 12544 | bytes 100352 | tf_op jit(solution)/shard_map/psum | solution.py:204
  (1221 shorter events, 272.6 us)
Async XLA Ops:
  7.2 924.1 %all-reduce.3.cloned.1.call-start = ((), (), s32[]{:S(2)}) async-start(), calls=%async_computation | async-start | bytes 4194304 | tf_op jit(solution)/shard_map/psum | solution.py:204
  8.0 6.1 collective-permute-start.5
  12.8 5.2 collective-permute-start.6
  18.9 8.5 collective-permute-start.7
  24.0 5.4 collective-permute-start.8
  39.1 41.8 %copy-start.91 = (f32[1,1,256]{2,1,0:T(1,128)}, f32[1,1,256]{2,1,0:T(1,128)S(1)}, u32[]{:S(2)}) copy-start(f32[1,1,256]{2,1,0:T(1,128)S(1)} %get-tuple-element.1519) | copy-start | bytes 3076 | tf_op jit(solution)/shard_map/while
  84.2 11.5 %collective-permute-start = (bf16[3,16,256]{2,1,0:T(8,128)(2,1)}, bf16[3,16,256]{2,1,0:T(8,128)(2,1)}, u32[]{:S(2)}, u32[]{:S(2)}) collective-permute-start(bf16[3,16,256]{2,1,0:T(8,128)(2,1)} %bitcast.412), channel_id=1, source_target_pairs={{16,0},{32,16},{48,32},{64,48},{80,64},{96,80},{112,96},{17,1},{33... | collective-permute-start | bytes 73736 | tf_op jit(solution)/shard_map/while/body/eval_jaxpr/ppermute | solution.py:19
  86.2 9.5 %collective-permute-start.1 = (bf16[3,16,256]{2,1,0:T(8,128)(2,1)}, bf16[3,16,256]{2,1,0:T(8,128)(2,1)}, u32[]{:S(2)}, u32[]{:S(2)}) collective-permute-start(bf16[3,16,256]{2,1,0:T(8,128)(2,1)} %bitcast.346), channel_id=1, source_target_pairs={{0,16},{16,32},{32,48},{48,64},{64,80},{80,96},{96,112},{1,17},{17... | collective-permute-start | bytes 73736 | tf_op jit(solution)/shard_map/while/body/eval_jaxpr/ppermute | solution.py:16
  96.5 7.0 collective-permute-start.2
  98.4 5.1 collective-permute-start.3
  108.6 6.5 collective-permute-start.4
  124.4 41.8 %copy-start.91 = (f32[1,1,256]{2,1,0:T(1,128)}, f32[1,1,256]{2,1,0:T(1,128)S(1)}, u32[]{:S(2)}) copy-start(f32[1,1,256]{2,1,0:T(1,128)S(1)} %get-tuple-element.1519) | copy-start | bytes 3076 | tf_op jit(solution)/shard_map/while
  169.5 13.3 %collective-permute-start = (bf16[3,16,256]{2,1,0:T(8,128)(2,1)}, bf16[3,16,256]{2,1,0:T(8,128)(2,1)}, u32[]{:S(2)}, u32[]{:S(2)}) collective-permute-start(bf16[3,16,256]{2,1,0:T(8,128)(2,1)} %bitcast.412), channel_id=1, source_target_pairs={{16,0},{32,16},{48,32},{64,48},{80,64},{96,80},{112,96},{17,1},{33... | collective-permute-start | bytes 73736 | tf_op jit(solution)/shard_map/while/body/eval_jaxpr/ppermute | solution.py:19
  171.5 11.3 %collective-permute-start.1 = (bf16[3,16,256]{2,1,0:T(8,128)(2,1)}, bf16[3,16,256]{2,1,0:T(8,128)(2,1)}, u32[]{:S(2)}, u32[]{:S(2)}) collective-permute-start(bf16[3,16,256]{2,1,0:T(8,128)(2,1)} %bitcast.346), channel_id=1, source_target_pairs={{0,16},{16,32},{32,48},{48,64},{64,80},{80,96},{96,112},{1,17},{17... | collective-permute-start | bytes 73736 | tf_op jit(solution)/shard_map/while/body/eval_jaxpr/ppermute | solution.py:16
  183.6 8.2 collective-permute-start.2
  185.7 6.1 collective-permute-start.3
  196.9 5.8 collective-permute-start.4
  212.1 41.8 %copy-start.91 = (f32[1,1,256]{2,1,0:T(1,128)}, f32[1,1,256]{2,1,0:T(1,128)S(1)}, u32[]{:S(2)}) copy-start(f32[1,1,256]{2,1,0:T(1,128)S(1)} %get-tuple-element.1519) | copy-start | bytes 3076 | tf_op jit(solution)/shard_map/while
  257.2 13.0 %collective-permute-start = (bf16[3,16,256]{2,1,0:T(8,128)(2,1)}, bf16[3,16,256]{2,1,0:T(8,128)(2,1)}, u32[]{:S(2)}, u32[]{:S(2)}) collective-permute-start(bf16[3,16,256]{2,1,0:T(8,128)(2,1)} %bitcast.412), channel_id=1, source_target_pairs={{16,0},{32,16},{48,32},{64,48},{80,64},{96,80},{112,96},{17,1},{33... | collective-permute-start | bytes 73736 | tf_op jit(solution)/shard_map/while/body/eval_jaxpr/ppermute | solution.py:19
  259.2 11.0 %collective-permute-start.1 = (bf16[3,16,256]{2,1,0:T(8,128)(2,1)}, bf16[3,16,256]{2,1,0:T(8,128)(2,1)}, u32[]{:S(2)}, u32[]{:S(2)}) collective-permute-start(bf16[3,16,256]{2,1,0:T(8,128)(2,1)} %bitcast.346), channel_id=1, source_target_pairs={{0,16},{16,32},{32,48},{48,64},{64,80},{80,96},{96,112},{1,17},{17... | collective-permute-start | bytes 73736 | tf_op jit(solution)/shard_map/while/body/eval_jaxpr/ppermute | solution.py:16
  271.0 8.8 collective-permute-start.2
  272.9 6.9 collective-permute-start.3
  284.9 50.8 %copy-start.14 = (bf16[1,16,16,256]{3,2,1,0:T(8,128)(2,1)}, bf16[1,16,16,256]{3,2,1,0:T(8,128)(2,1)S(1)}, u32[]{:S(2)}) copy-start(bf16[1,16,16,256]{3,2,1,0:T(8,128)(2,1)S(1)} %get-tuple-element.1708) | copy-start | bytes 393220 | tf_op jit(solution)/shard_map/while
  284.9 50.8 %copy-start.12 = (bf16[1,16,16,256]{3,2,1,0:T(8,128)(2,1)S(1)}, bf16[1,16,16,256]{3,2,1,0:T(8,128)(2,1)}, u32[]{:S(2)}) copy-start(bf16[1,16,16,256]{3,2,1,0:T(8,128)(2,1)} %get-tuple-element.1755) | copy-start | bytes 393220 | tf_op jit(solution)/shard_map/while
  284.9 50.8 %collective-permute-start.4 = (bf16[16,16,256]{2,1,0:T(8,128)(2,1)S(1)}, bf16[16,16,256]{2,1,0:T(8,128)(2,1)S(1)}, u32[]{:S(2)}, u32[]{:S(2)}) collective-permute-start(bf16[16,16,256]{2,1,0:T(8,128)(2,1)S(1)} %get-tuple-element.1605), channel_id=1, source_target_pairs={{128,0},{256,128},{384,256},{129,1},{257,129},{385,257},{130,2},{2... | collective-permute-start | bytes 393224 | tf_op jit(solution)/shard_map/while/body/eval_jaxpr/ppermute | solution.py:27
  286.4 49.3 %copy-start.16 = (f32[7,7,256]{2,1,0:T(8,128)}, f32[7,7,256]{2,1,0:T(8,128)S(1)}, u32[]{:S(2)}) copy-start(f32[7,7,256]{2,1,0:T(8,128)S(1)} %select_add_fusion.8) | copy-start | bytes 150532 | tf_op jit(solution)/shard_map/while
  286.4 49.3 %copy-start.116 = (f32[1,1024]{1,0:T(1,128)S(1)}, f32[1,1024]{1,0:T(1,128)}, u32[]{:S(2)}) copy-start(f32[1,1024]{1,0:T(1,128)} %get-tuple-element.1819) | copy-start | bytes 12292 | tf_op jit(solution)/shard_map/while
  405.6 12.7 %collective-permute-start = (bf16[3,16,256]{2,1,0:T(8,128)(2,1)}, bf16[3,16,256]{2,1,0:T(8,128)(2,1)}, u32[]{:S(2)}, u32[]{:S(2)}) collective-permute-start(bf16[3,16,256]{2,1,0:T(8,128)(2,1)} %bitcast.412), channel_id=1, source_target_pairs={{16,0},{32,16},{48,32},{64,48},{80,64},{96,80},{112,96},{17,1},{33... | collective-permute-start | bytes 73736 | tf_op jit(solution)/shard_map/while/body/eval_jaxpr/ppermute | solution.py:19
  407.6 10.7 %collective-permute-start.1 = (bf16[3,16,256]{2,1,0:T(8,128)(2,1)}, bf16[3,16,256]{2,1,0:T(8,128)(2,1)}, u32[]{:S(2)}, u32[]{:S(2)}) collective-permute-start(bf16[3,16,256]{2,1,0:T(8,128)(2,1)} %bitcast.346), channel_id=1, source_target_pairs={{0,16},{16,32},{32,48},{48,64},{64,80},{80,96},{96,112},{1,17},{17... | collective-permute-start | bytes 73736 | tf_op jit(solution)/shard_map/while/body/eval_jaxpr/ppermute | solution.py:16
  419.2 8.8 collective-permute-start.2
  421.1 6.9 collective-permute-start.3
  433.1 5.8 collective-permute-start.4
  (434 other events, 3393.1 us)
Sparse Core Ops, SparseCore 0:
  440.7 210.1 all-reduce.2
where the time goes:
time: 947 us; the launch traced here: 941 us
  blocking collectives  490 us (52%)
  local copies, waits for them, and re-layouts  207 us (22%)
  other arithmetic  78.1 us (8%)
  starting transfers between devices  72.9 us (8%)
  waiting for transfers between devices  68.8 us (7%)
  between operations  14.8 us (2%)
    psum x1, blocking collectives, per_device(): lax.psum((sum_in, sum_out, sum_taps), ('row', 'col'))  490 us
    mul x188, local copies, waits for them, and re-layouts, depthwise(): conv_taps[shift_r, shift_c]  157 us
    ppermute x4, waiting for transfers between devices, shifted(): return lax.ppermute(block, axis, route)  63 us
    ppermute x10, starting transfers between devices, with_halo(): lax.ppermute(lax.slice_in_dim(block, block.shape[dim] - width, None, axis...  50.8 us
    convert_element_type x12, other arithmetic, depthwise(): total = total + conv_taps[shift_r, shift_c] * padded[shift_r:shift_r + he...  25 us
  transfers between devices with their start and end apart: 25, of which 6 were waited for; matrix products, arithmetic and copies ran while one was open for 3% of the time, Pallas kernels for 0%

commit v1 on v0

v1 whole, which is shorter than its diff:
```python
import functools
import math

import jax
import jax.numpy as jnp
from jax import lax
from jax.experimental import pallas as pl
from jax.experimental.pallas import tpu as pltpu
from jax.sharding import PartitionSpec as P

F32 = jnp.float32
BF16 = jnp.bfloat16
MESH = pl.DeviceIdType.MESH
EPS = 1e-06
H = 16
W = 16
C = 256
HID = 1024
ROWS = 8
COLS = 16
YS = 8
SEGS = 4
LEFT = 8
PADW = 32
CONV_ROWS = 4
CHUNKS = 2
CH_ROWS = H // CHUNKS
CH_PIX = CH_ROWS * W
DIRS = ((-1, 0), (1, 0), (0, -1), (0, 1), (-1, -1), (-1, 1), (1, -1), (1, 1))
BACK = (1, 0, 3, 2, 7, 6, 5, 4)
GELU_A = math.sqrt(2.0 / math.pi)
GELU_B = 0.044715
NT = (((1,), (1,)), ((), ()))
TN = (((0,), (0,)), ((), ()))


def conv_rows(pad, taps, row0, flip):
    halves = []
    for h in range(2):
        acc = jnp.zeros((CONV_ROWS, W, 128), F32)
        for j in range(7):
            window = pad[h, pl.ds(row0, CONV_ROWS + 6), LEFT - 3 + j : LEFT - 3 + j + W, :]
            for i in range(7):
                ti, tj = (6 - i, 6 - j) if flip else (i, j)
                tap = taps[ti, tj : tj + 1, h * 128 : (h + 1) * 128]
                acc = acc + tap[None] * window[i : i + CONV_ROWS]
        halves.append(acc.reshape(CONV_ROWS * W, 128))
    return jnp.concatenate(halves, axis=-1)


def body(
    scale,
    saved, og, tissue, taps, cbias, gain, nbias, w_in, b_in, w_out, lscale,
    out, gi_out, go_out, taps_out,
    xpad, gpad, std, inv, nbuf, hbuf, dgelu, bgb, pgb, gin, cgt,
    col_s, row_r, col_r, cor_r,
    s0i, s0o, r0i, r0o, t1i, t1o, r1i, r1o, p2i, p2o, r2i, r2o, r3,
    tacc, ts0, tr0, try_, trz, tfin,
    halo_send, halo_recv, shift_send, shift_recv,
    sib_send, sib_recv, a_send, a_recv, b_send, b_recv,
    c_send, c_recv, d_send, d_recv, e_send, e_recv, ty_send, ty_recv, tz_send, tz_recv,
):
    seg = lax.axis_index("segment")
    r = lax.axis_index("row")
    c = lax.axis_index("col")
    core = lax.rem(c, 2)
    y = lax.div(c, 2)
    sib = (seg, r, c + 1 - 2 * core)
    off_c = c + 2 * core - 1
    off_ok = jnp.logical_and(off_c >= 0, off_c < COLS)

    def near_ok(d):
        dr, dc = DIRS[d]
        ok = None
        if dr:
            ok = (r > 0) if dr < 0 else (r < ROWS - 1)
        if dc:
            okc = (c > 0) if dc < 0 else (c < COLS - 1)
            ok = okc if ok is None else jnp.logical_and(ok, okc)
        return ok

    def near_id(d):
        dr, dc = DIRS[d]
        return (seg, r + dr, c + dc)

    def zpeer(k):
        return lax.rem(r + k, ROWS)

    def ypeer(k):
        return lax.rem(y + k, YS)

    barrier = pltpu.get_barrier_semaphore()

    def greet(device):
        pl.semaphore_signal(barrier, inc=1, device_id=device, device_id_type=MESH)

    greet(sib)
    count = 1 + 2 * 7
    for k in range(1, 8):
        greet((seg, zpeer(k), c))
        greet((seg, r, 2 * ypeer(k) + core))

    @pl.when(off_ok)
    def _():
        greet((seg, r, off_c))

    count = count + jnp.where(off_ok, 1, 0)
    for d in range(4, 8):
        ok = near_ok(d)

        @pl.when(ok)
        def _(d=d):
            greet(near_id(d))

        count = count + jnp.where(ok, 1, 0)

    @pl.when(seg > 0)
    def _():
        greet((seg - 1, r, c))

    @pl.when(seg < SEGS - 1)
    def _():
        greet((seg + 1, r, c))

    count = count + jnp.where(seg > 0, 1, 0) + jnp.where(seg < SEGS - 1, 1, 0)

    def stage_cols(pad, p):
        for h in range(2):
            lanes = slice(h * 128, (h + 1) * 128)
            col_s[p, 0, :, :, lanes] = pad[h, 3 : 3 + H, LEFT : LEFT + 3, :].astype(BF16)
            col_s[p, 1, :, :, lanes] = pad[h, 3 : 3 + H, LEFT + W - 3 : LEFT + W, :].astype(BF16)

    for h in range(2):
        xpad[h, 3 : 3 + H, LEFT : LEFT + W, :] = saved[:, :, h * 128 : (h + 1) * 128].astype(F32)
    stage_cols(xpad, 0)

    def landing(p, d):
        if d < 2:
            return row_r.at[p, d]
        if d < 4:
            return col_r.at[p, d - 2]
        return cor_r.at[p, d - 4]

    for p in range(2):
        for d in range(8):

            @pl.when(jnp.logical_not(near_ok(d)))
            def _(p=p, d=d):
                ref = landing(p, d)
                ref[...] = jnp.zeros(ref.shape, BF16)

    pl.semaphore_wait(barrier, count)

    def halo_copy(p, tile, d):
        dr, dc = DIRS[d]
        rows = slice(0, 3) if dr < 0 else slice(H - 3, H)
        if dc == 0:
            src = tile.at[rows]
        elif dr == 0:
            src = col_s.at[p, 0 if dc < 0 else 1]
        else:
            src = col_s.at[p, 0 if dc < 0 else 1, rows]
        return pltpu.make_async_remote_copy(
            src_ref=src,
            dst_ref=landing(p, BACK[d]),
            send_sem=halo_send.at[p, d],
            recv_sem=halo_recv.at[p, BACK[d]],
            device_id=near_id(d),
            device_id_type=MESH,
        )

    def halo_start(p, tile):
        for d in (4, 5, 6, 7, 0, 1, 2, 3):

            @pl.when(near_ok(d))
            def _(d=d):
                halo_copy(p, tile, d).start()

    def halo_wait(p, tile):
        for d in range(8):

            @pl.when(near_ok(d))
            def _(d=d):
                pltpu.make_async_remote_copy(
                    src_ref=landing(p, d),
                    dst_ref=landing(p, d),
                    send_sem=halo_send.at[p, d],
                    recv_sem=halo_recv.at[p, d],
                    device_id=near_id(d),
                    device_id_type=MESH,
                ).wait_recv()

    def halo_drain(p, tile):
        for d in range(8):

            @pl.when(near_ok(d))
            def _(d=d):
                halo_copy(p, tile, d).wait_send()

    def unpack(pad, p):
        for h in range(2):
            lanes = slice(h * 128, (h + 1) * 128)
            lo, hi = slice(LEFT - 3, LEFT), slice(LEFT + W, LEFT + W + 3)
            pad[h, 0:3, LEFT : LEFT + W, :] = row_r[p, 0, :, :, lanes].astype(F32)
            pad[h, 3 + H : 6 + H, LEFT : LEFT + W, :] = row_r[p, 1, :, :, lanes].astype(F32)
            pad[h, 3 : 3 + H, lo, :] = col_r[p, 0, :, :, lanes].astype(F32)
            pad[h, 3 : 3 + H, hi, :] = col_r[p, 1, :, :, lanes].astype(F32)
            pad[h, 0:3, lo, :] = cor_r[p, 0, :, :, lanes].astype(F32)
            pad[h, 0:3, hi, :] = cor_r[p, 1, :, :, lanes].astype(F32)
            pad[h, 3 + H : 6 + H, lo, :] = cor_r[p, 2, :, :, lanes].astype(F32)
            pad[h, 3 + H : 6 + H, hi, :] = cor_r[p, 3, :, :, lanes].astype(F32)

    halo_start(0, saved)
    halo_wait(0, saved)
    unpack(xpad, 0)

    @pl.loop(0, H // CONV_ROWS)
    def _(n):
        conv = conv_rows(xpad, taps, n * CONV_ROWS, False) + cbias[...]
        pix = pl.ds(pl.multiple_of(n * (CONV_ROWS * W), CONV_ROWS * W), CONV_ROWS * W)
        centred = conv - jnp.mean(conv, axis=-1, keepdims=True)
        inv_std = lax.rsqrt(jnp.mean(centred * centred, axis=-1, keepdims=True) + EPS)
        standard = centred * inv_std
        std[pix, :] = standard
        inv[pix, :] = jnp.broadcast_to(inv_std, (CONV_ROWS * W, 128))
        nbuf[pix, :] = (standard * gain[...] + nbias[...]).astype(BF16)

    @pl.loop(0, HID // 256)
    def _(n):
        units = pl.ds(pl.multiple_of(n * 256, 256), 256)
        pre = jnp.dot(nbuf[...], w_in[:, units], preferred_element_type=F32) + b_in[:, units]
        square = pre * pre
        th = jnp.tanh(GELU_A * (pre + GELU_B * (square * pre)))
        half = 0.5 * (1.0 + th)
        hbuf[:, units] = (pre * half).astype(BF16)
        slope = GELU_A * (1.0 + (3.0 * GELU_B) * square)
        dgelu[:, units] = half + 0.5 * pre * (1.0 - th * th) * slope

    def shift_copy(src, n):
        rows = pl.ds(n * CH_ROWS, CH_ROWS)
        return pltpu.make_async_remote_copy(
            src_ref=src.at[rows],
            dst_ref=gin.at[rows],
            send_sem=shift_send.at[n],
            recv_sem=shift_recv.at[n],
            device_id=(lax.rem(seg + SEGS - 1, SEGS), r, c),
            device_id_type=MESH,
        )

    mask = tissue[0, 0].astype(F32)

    @pl.when(seg == SEGS - 1)
    def _():
        gin[...] = og[...]

    for n in range(CHUNKS):

        @pl.when(seg < SEGS - 1)
        def _(n=n):
            shift_copy(out, n).wait_recv()

        rows = slice(n * CH_ROWS, (n + 1) * CH_ROWS)
        pix = slice(n * CH_PIX, (n + 1) * CH_PIX)
        upstream = gin[rows].reshape(CH_PIX, C).astype(F32)
        bg = (mask * lscale[...] * upstream).astype(BF16)
        bgb[pix, :] = bg
        hidden_grad = lax.dot_general(bg, w_out[...], NT, preferred_element_type=F32)
        pg = (hidden_grad * dgelu[pix, :]).astype(BF16)
        pgb[pix, :] = pg
        ng = lax.dot_general(pg, w_in[...], NT, preferred_element_type=F32) * gain[...]
        standard = std[pix, :]
        m1 = jnp.mean(ng, axis=-1, keepdims=True)
        m2 = jnp.mean(ng * standard, axis=-1, keepdims=True)
        cg = (inv[pix, 0:1] * (ng - m1 - standard * m2)).astype(BF16)
        cgt[rows] = cg.reshape(CH_ROWS, W, C)
        wide = cg.astype(F32).reshape(CH_ROWS, W, C)
        for h in range(2):
            gpad[h, 3 + n * CH_ROWS : 3 + (n + 1) * CH_ROWS, LEFT : LEFT + W, :] = wide[:, :, h * 128 : (h + 1) * 128]
    stage_cols(gpad, 1)
    halo_start(1, cgt)

    for n in range(HID // 256):
        units = slice(n * 256, (n + 1) * 256)
        gi = lax.dot_general(nbuf[...], pgb[:, units], TN, preferred_element_type=F32) * scale
        go = lax.dot_general(hbuf[:, units], bgb[...], TN, preferred_element_type=F32) * scale
        gi = gi.astype(BF16)
        go = go.astype(BF16)
        for k in range(COLS):
            s0i[k % 2, k // 2, :, units] = gi[16 * k : 16 * k + 16]
        for k in range(4):
            owner = n * 4 + k
            s0o[owner % 2, owner // 2] = go[64 * k : 64 * k + 64]

    def sib_copy(src, dst, k):
        return pltpu.make_async_remote_copy(
            src_ref=src, dst_ref=dst, send_sem=sib_send.at[k], recv_sem=sib_recv.at[k],
            device_id=sib, device_id_type=MESH,
        )

    other = 1 - core
    first_i = sib_copy(s0i.at[other], r0i, 0)
    first_o = sib_copy(s0o.at[other], r0o, 1)
    first_i.start()
    first_o.start()

    halo_wait(1, cgt)
    unpack(gpad, 1)
    for n in range(CHUNKS):
        for m in range(CH_ROWS // CONV_ROWS):
            row0 = n * CH_ROWS + m * CONV_ROWS
            total = conv_rows(gpad, taps, row0, True).reshape(CONV_ROWS, W, C)
            total = gin[row0 : row0 + CONV_ROWS].astype(F32) + total
            out[row0 : row0 + CONV_ROWS] = total.astype(BF16)

        @pl.when(seg > 0)
        def _(n=n):
            shift_copy(out, n).start()

    def remote(src, dst, send, recv, device):
        return pltpu.make_async_remote_copy(
            src_ref=src, dst_ref=dst, send_sem=send, recv_sem=recv,
            device_id=device, device_id_type=MESH,
        )

    first_i.wait()
    for k in range(YS):
        t1i[k] = (s0i[core, k].astype(F32) + r0i[k].astype(F32)).astype(BF16)

    def a_copy(k):
        p = ypeer(k)
        return remote(t1i.at[p], r1i.at[k - 1], a_send.at[k - 1], a_recv.at[k - 1], (seg, r, 2 * p + core))

    for k in range(1, 8):
        a_copy(k).start()
    first_o.wait()
    for k in range(YS):
        both = s0o[core, k].astype(F32) + r0o[k].astype(F32)
        both = both.astype(BF16)
        for q in range(ROWS):
            t1o[q, k] = both[16 * (q // 2) : 16 * (q // 2) + 16, 128 * (q % 2) : 128 * (q % 2) + 128]

    def b_copy(k):
        p = zpeer(k)
        return remote(t1o.at[p], r1o.at[k - 1], b_send.at[k - 1], b_recv.at[k - 1], (seg, p, c))

    for k in range(1, 8):
        b_copy(k).start()

    for h in range(2):
        for j in range(7):
            sums = [jnp.zeros((8, 128), F32) for _ in range(7)]
            for block in range(H // CONV_ROWS):
                row0 = block * CONV_ROWS
                window = xpad[h, row0 : row0 + CONV_ROWS + 6, LEFT - 3 + j : LEFT - 3 + j + W, :]
                grad = gpad[h, 3 + row0 : 3 + row0 + CONV_ROWS, LEFT : LEFT + W, :]
                for i in range(7):
                    prod = (window[i : i + CONV_ROWS] * grad).reshape(2 * CONV_ROWS, 8, 128)
                    sums[i] = sums[i] + jnp.sum(prod, axis=0)
            for i in range(7):
                tacc[h, 7 * i + j] = sums[i]
    for h in range(2):
        ts0[h] = jnp.zeros((64, 128), BF16)
        ts0[h, 0:49] = (jnp.sum(tacc[h], axis=1) * scale).astype(BF16)
    tap_a = sib_copy(ts0.at[other], tr0, 2)
    tap_a.start()

    for k in range(1, 8):
        a_copy(k).wait_recv()
    mine = t1i[y].astype(F32)
    for k in range(7):
        mine = mine + r1i[k].astype(F32)
    mine = mine.astype(BF16)
    for q in range(ROWS):
        p2i[q] = mine[:, 128 * q : 128 * q + 128]

    def c_copy(k):
        p = zpeer(k)
        return remote(p2i.at[p], r2i.at[k - 1], c_send.at[k - 1], c_recv.at[k - 1], (seg, p, c))

    for k in range(1, 8):
        c_copy(k).start()

    tap_a.wait()
    try_[y] = (ts0[core].astype(F32) + tr0[...].astype(F32)).astype(BF16)

    def ty_copy(k):
        return remote(try_.at[y], try_.at[y], ty_send.at[k - 1], ty_recv.at[y], (seg, r, 2 * ypeer(k) + core))

    def ty_landed(k):
        p = ypeer(k)
        return remote(try_.at[p], try_.at[p], ty_send.at[k - 1], ty_recv.at[p], (seg, r, 2 * p + core))

    for k in range(1, 8):
        ty_copy(k).start()

    for k in range(1, 8):
        b_copy(k).wait_recv()
    part = t1o[r].astype(F32)
    for k in range(7):
        part = part + r1o[k].astype(F32)
    p2o[...] = part.astype(BF16)

    def d_copy(k):
        p = ypeer(k)
        return remote(p2o.at[p], r2o.at[k - 1], d_send.at[k - 1], d_recv.at[k - 1], (seg, r, 2 * p + core))

    for k in range(1, 8):
        d_copy(k).start()

    for k in range(1, 8):
        ty_landed(k).wait_recv()
    tsum = try_[0].astype(F32)
    for k in range(1, 8):
        tsum = tsum + try_[k].astype(F32)
    trz[r] = tsum.astype(BF16)

    def tz_copy(k):
        return remote(trz.at[r], trz.at[r], tz_send.at[k - 1], tz_recv.at[r], (seg, zpeer(k), c))

    def tz_landed(k):
        p = zpeer(k)
        return remote(trz.at[p], trz.at[p], tz_send.at[k - 1], tz_recv.at[p], (seg, p, c))

    for k in range(1, 8):
        tz_copy(k).start()

    for k in range(1, 8):
        c_copy(k).wait_recv()
    full_i = p2i[r].astype(F32)
    for k in range(7):
        full_i = full_i + r2i[k].astype(F32)
    for k in range(1, 8):
        d_copy(k).wait_recv()
    full_o = p2o[y].astype(F32)
    for k in range(7):
        full_o = full_o + r2o[k].astype(F32)
    r3[r, 0] = full_i
    r3[r, 1] = full_o

    def e_copy(k):
        return remote(r3.at[r], r3.at[r], e_send.at[k - 1], e_recv.at[r], (seg, zpeer(k), c))

    def e_landed(k):
        p = zpeer(k)
        return remote(r3.at[p], r3.at[p], e_send.at[k - 1], e_recv.at[p], (seg, p, c))

    for k in range(1, 8):
        e_copy(k).start()

    for k in range(1, 8):
        tz_landed(k).wait_recv()
    tsum = trz[0].astype(F32)
    for k in range(1, 8):
        tsum = tsum + trz[k].astype(F32)
    tfin[core] = tsum
    tap_b = sib_copy(tfin.at[core], tfin.at[core], 3)
    tap_b.start()

    for k in range(1, 8):
        e_landed(k).wait_recv()
    for q in range(ROWS):
        gi_out[:, 128 * q : 128 * q + 128] = r3[q, 0]
        go_out[16 * (q // 2) : 16 * (q // 2) + 16, 128 * (q % 2) : 128 * (q % 2) + 128] = r3[q, 1]

    tap_b.wait_send()
    sib_copy(tfin.at[other], tfin.at[other], 3).wait_recv()
    for h in range(2):
        for i in range(7):
            taps_out[i, :, h * 128 : (h + 1) * 128] = tfin[h, 7 * i : 7 * i + 7, :]

    halo_drain(0, saved)
    halo_drain(1, cgt)
    for n in range(CHUNKS):

        @pl.when(seg > 0)
        def _(n=n):
            shift_copy(out, n).wait_send()

    for k in range(1, 8):
        for copy in (a_copy, b_copy, c_copy, d_copy, e_copy, ty_copy, tz_copy):
            copy(k).wait_send()


def per_device(
    saved_inputs, out_grad, tissue, conv_taps, conv_bias, norm_gain, norm_bias,
    w_in, b_in, w_out, layer_scale,
):
    scale = 1.0 / math.sqrt(ROWS * H * COLS * W)
    vmem = pl.BlockSpec(memory_space=pltpu.VMEM)
    smem = pl.BlockSpec(memory_space=pltpu.SMEM)
    dma = pltpu.SemaphoreType.DMA
    px = H * W
    out, gi, go, gt = pl.pallas_call(
        functools.partial(body, scale),
        out_shape=(
            jax.ShapeDtypeStruct((H, W, C), BF16),
            jax.ShapeDtypeStruct((C // COLS, HID), F32),
            jax.ShapeDtypeStruct((HID // COLS, C), F32),
            jax.ShapeDtypeStruct((7, 7, C), F32),
        ),
        in_specs=[vmem, vmem, smem] + [vmem] * 8,
        out_specs=(vmem, vmem, vmem, vmem),
        scratch_shapes=[
            pltpu.VMEM((2, H + 6, PADW, 128), F32),
            pltpu.VMEM((2, H + 6, PADW, 128), F32),
            pltpu.VMEM((px, C), F32),
            pltpu.VMEM((px, 128), F32),
            pltpu.VMEM((px, C), BF16),
            pltpu.VMEM((px, HID), BF16),
            pltpu.VMEM((px, HID), F32),
            pltpu.VMEM((px, C), BF16),
            pltpu.VMEM((px, HID), BF16),
            pltpu.VMEM((H, W, C), BF16),
            pltpu.VMEM((H, W, C), BF16),
            pltpu.VMEM((2, 2, H, 3, C), BF16),
            pltpu.VMEM((2, 2, 3, W, C), BF16),
            pltpu.VMEM((2, 2, H, 3, C), BF16),
            pltpu.VMEM((2, 4, 3, 3, C), BF16),
            pltpu.VMEM((2, YS, 16, HID), BF16),
            pltpu.VMEM((2, YS, 64, C), BF16),
            pltpu.VMEM((YS, 16, HID), BF16),
            pltpu.VMEM((YS, 64, C), BF16),
            pltpu.VMEM((YS, 16, HID), BF16),
            pltpu.VMEM((ROWS, YS, 16, 128), BF16),
            pltpu.VMEM((7, 16, HID), BF16),
            pltpu.VMEM((7, YS, 16, 128), BF16),
            pltpu.VMEM((ROWS, 16, 128), BF16),
            pltpu.VMEM((YS, 16, 128), BF16),
            pltpu.VMEM((7, 16, 128), BF16),
            pltpu.VMEM((7, 16, 128), BF16),
            pltpu.VMEM((ROWS, 2, 16, 128), F32),
            pltpu.VMEM((2, 49, 8, 128), F32),
            pltpu.VMEM((2, 64, 128), BF16),
            pltpu.VMEM((64, 128), BF16),
            pltpu.VMEM((YS, 64, 128), BF16),
            pltpu.VMEM((ROWS, 64, 128), BF16),
            pltpu.VMEM((2, 64, 128), F32),
            dma((2, 8)), dma((2, 8)), dma((CHUNKS,)), dma((CHUNKS,)),
            dma((4,)), dma((4,)),
            dma((7,)), dma((7,)), dma((7,)), dma((7,)),
            dma((7,)), dma((7,)), dma((7,)), dma((7,)),
            dma((7,)), dma((8,)), dma((7,)), dma((8,)), dma((7,)), dma((8,)),
        ],
        compiler_params=pltpu.CompilerParams(collective_id=0, has_side_effects=True),
    )(
        saved_inputs[0, 0], out_grad[0], tissue[0], conv_taps[0], conv_bias, norm_gain, norm_bias,
        w_in[0], b_in, w_out[0], layer_scale,
    )
    return (out[None, None], gi[None], go[None], gt[None])


def solution(mesh):
    return jax.shard_map(
        per_device,
        mesh=mesh,
        in_specs=(
            P("segment", None, "row", "col", None),
            P(None, "row", "col", None),
            P(None, "row", "col"),
            P("segment", None, None, None),
            P("segment", None),
            P("segment", None),
            P("segment", None),
            P("segment", None, None),
            P("segment", None),
            P("segment", None, None),
            P("segment", None),
        ),
        out_specs=(
            P("segment", None, "row", "col", None),
            P("segment", "col", None),
            P("segment", "col", None),
            P("segment", None, None, None),
        ),
        check_vma=False,
    )
```

time: 947 us -> 90.3 us (0.10)
  blocking collectives: 490 us -> 0 us
  local copies, waits for them, and re-layouts: 207 us -> 6.02 us
  Pallas kernels: 0 us -> 82.7 us
  other arithmetic: 78.1 us -> 0 us
  starting transfers between devices: 72.9 us -> 0 us
  waiting for transfers between devices: 68.8 us -> 0 us
  between operations: 14.8 us -> 1.29 us
    psum x1 -> x0, blocking collectives: 490 us -> none  [per_device(): lax.psum((sum_in, sum_out, sum_taps), ('row', 'col'))]
    mul x192 -> x0, local copies, waits for them, and re-layouts: 163 us -> none  [the longest x188 157 us: depthwise(): conv_taps[shift_r, shift_c]]
    pallas_call x0 -> x1, Pallas kernels: none -> 82.7 us  [per_device(): pl.pallas_call(functools.partial(body, scale), out_shape=(jax.ShapeDtypeS...]
    ppermute x24 -> x0, starting transfers between devices: 72.9 us -> none  [the longest x10 50.8 us: with_halo(): lax.ppermute(lax.slice_in_dim(block, block.shape[dim] - width, None, axis...]
    ppermute x24 -> x0, waiting for transfers between devices: 68.8 us -> none  [the longest x4 63 us: shifted(): return lax.ppermute(block, axis, route)]
    convert_element_type x14 -> x0, other arithmetic: 25.7 us -> none  [the longest x12 25 us: depthwise(): total = total + conv_taps[shift_r, shift_c] * padded[shift_r:shift_r + he...]
    slice x25 -> x0, local copies, waits for them, and re-layouts: 25.1 us -> none  [the longest x12 14.9 us: depthwise(): conv_taps[shift_r, shift_c]]
    reduce_sum x14 -> x0, other arithmetic: 17.9 us -> none  [the longest x1 9.61 us: normalize(): average = jnp.mean(conv_out, axis=-1, keepdims=True)]
  transfers between devices with their start and end apart: 25 -> 0, of which waited for: 6 -> 0; matrix products, arithmetic and copies ran while one was open for 3% -> 0% of each run, Pallas kernels for 0% -> 0%
where the time goes in v1:
time: 90.3 us; the launch traced here: 90 us
  Pallas kernels  82.7 us (92%)
  local copies, waits for them, and re-layouts  6.02 us (7%)
  between operations  1.29 us (1%)
    pallas_call x1, Pallas kernels, per_device(): pl.pallas_call(functools.partial(body, scale), out_shape=(jax.ShapeDtypeS...  82.7 us
    unnamed x9, local copies, waits for them, and re-layouts  6.02 us

profile of v1, /device:TPU:1, one launch (start us, length us, event | category | flops | bytes accessed | tf_op | source)
XLA Modules:
  0.0 90.0 jit_solution(17392143416169318368)
XLA Ops:
  1.3 1.4 %copy.18 = f32[1,7,7,256]{3,2,0,1:T(8,128)} copy(f32[1,7,7,256]{3,0,2,1:T(1,128)} %param.14) | data formatting | bytes 100352
  2.7 82.7 %shard_map.138 = (bf16[16,16,256]{2,1,0:T(8,128)(2,1)}, f32[16,1024]{1,0:T(8,128)}, f32[64,256]{1,0:T(8,128)}, f32[7,7,256]{2,1,0:T(8,128)}) custom-call(bf16[16,16,256]{2,1,0:T(8,128)(2,1)} %bitcast.16, bf16[16,16,256]{2,1,0:T(8,128)(2,1)} %bitcast.17, s32[1,1]{1,0:T(1,128)} %bitcast.12.tissue, f32[7,7,256]{2,1,0:T(8,128)} %bitcast.15, f32[1,256]{1,0:T(1,128)} %cbias.1, ...), custom_call_target="tpu_custom_call" | custom-call | tf_op jit(solution)/shard_map/pallas_call | solution.py:493
  85.4 1.5 %copy.15 = f32[1,7,7,256]{3,0,2,1:T(1,128)} copy(f32[1,7,7,256]{3,2,1,0:T(8,128)} %bitcast.21) | data formatting | bytes 100352
  86.9 0.0 copy-start.1
  86.9 1.6 %copy.23 = bf16[1,1,16,16,256]{4,3,2,1,0:T(8,128)(2,1)} copy(bf16[1,1,16,16,256]{4,3,2,1,0:T(8,128)(2,1)} %bitcast.18) | data formatting | bytes 262144
  88.5 0.0 copy-done.1
  88.5 0.0 copy-start
  88.5 0.6 copy.24
  89.1 0.2 copy-done
  89.4 0.6 copy.25
Async XLA Ops:
  86.9 1.6 %copy-start.1 = (f32[16,1024]{1,0:T(8,128)S(1)}, f32[16,1024]{1,0:T(8,128)}, u32[]{:S(2)}) copy-start(f32[16,1024]{1,0:T(8,128)} %get-tuple-element.9) | copy-start | bytes 196612
  88.5 0.9 copy-start

commit v2 on v1

v2 whole, which is shorter than its diff:
```python
import functools
import math

import jax
import jax.numpy as jnp
from jax import lax
from jax.experimental import pallas as pl
from jax.experimental.pallas import tpu as pltpu
from jax.sharding import PartitionSpec as P

F32 = jnp.float32
BF16 = jnp.bfloat16
MESH = pl.DeviceIdType.MESH
EPS = 1e-06
VMEM_MAIN = 28 * 1024 * 1024
H = 16
W = 16
C = 256
HID = 1024
ROWS = 8
COLS = 16
YS = 8
SEGS = 4
LEFT = 8
PADW = 32
CONV_ROWS = 4
ORDER = (0, 12, 4, 8)
CHUNKS = len(ORDER)
CH_PIX = CONV_ROWS * W
DIRS = ((-1, 0), (1, 0), (0, -1), (0, 1), (-1, -1), (-1, 1), (1, -1), (1, 1))
BACK = (1, 0, 3, 2, 7, 6, 5, 4)
FAR = (4, 3, 5, 2, 6, 1, 7)
GELU_A = math.sqrt(2.0 / math.pi)
GELU_B = 0.044715
NT = (((1,), (1,)), ((), ()))
TN = (((0,), (0,)), ((), ()))


def conv_rows(pad, taps, row0, flip):
    halves = []
    for h in range(2):
        acc = jnp.zeros((CONV_ROWS, W, 128), F32)
        for j in range(7):
            window = pad[h, pl.ds(row0, CONV_ROWS + 6), LEFT - 3 + j : LEFT - 3 + j + W, :]
            for i in range(7):
                ti, tj = (6 - i, 6 - j) if flip else (i, j)
                tap = taps[ti, tj, :, h * 128 : (h + 1) * 128]
                acc = acc + tap[None] * window[i : i + CONV_ROWS]
        halves.append(acc.reshape(CONV_ROWS * W, 128))
    return jnp.concatenate(halves, axis=-1)


def body(
    scale,
    saved_h, og_h, tissue_h, taps_h, cbias_h, gain_h, nbias_h, w_in_h, b_in_h, w_out_h, lscale_h,
    out, gi_out, go_out, taps_out,
    saved, og, tissue, taps, cbias, gain, nbias, w_in, b_in, w_out, lscale, load_sem, tbuf, htbuf,
    xpad, gpad, std, inv, nbuf, hbuf, dgelu, bgb, pgb, gin, cgt,
    col_s, row_r, col_r, cor_r, strip, corner,
    s0i, s0o, r0i, r0o, t1i, t1o, r1i, r1o, p2i, p2o, r2i, r2o, r3,
    tacc, ts0, tr0, try_, trz, tfin,
    halo_send, halo_recv, shift_send, shift_recv,
    sib_send, sib_recv, a_send, a_recv, b_send, b_recv,
    c_send, c_recv, d_send, d_recv, e_send, e_recv, ty_send, ty_recv, tz_send, tz_recv,
):
    seg = lax.axis_index("segment")
    r = lax.axis_index("row")
    c = lax.axis_index("col")
    core = lax.rem(c, 2)
    y = lax.div(c, 2)
    sib = (seg, r, c + 1 - 2 * core)
    off_c = c + 2 * core - 1
    off_ok = jnp.logical_and(off_c >= 0, off_c < COLS)

    def near_ok(d):
        dr, dc = DIRS[d]
        ok = None
        if dr:
            ok = (r > 0) if dr < 0 else (r < ROWS - 1)
        if dc:
            okc = (c > 0) if dc < 0 else (c < COLS - 1)
            ok = okc if ok is None else jnp.logical_and(ok, okc)
        return ok

    def near_id(d):
        dr, dc = DIRS[d]
        return (seg, r + dr, c + dc)

    def zpeer(k):
        return lax.rem(r + k, ROWS)

    def ypeer(k):
        return lax.rem(y + k, YS)

    barrier = pltpu.get_barrier_semaphore()

    def greet(device):
        pl.semaphore_signal(barrier, inc=1, device_id=device, device_id_type=MESH)

    greet(sib)
    count = 1 + 2 * 7
    for k in range(1, 8):
        greet((seg, zpeer(k), c))
        greet((seg, r, 2 * ypeer(k) + core))

    @pl.when(off_ok)
    def _():
        greet((seg, r, off_c))

    count = count + jnp.where(off_ok, 1, 0)
    for d in range(4, 8):
        ok = near_ok(d)

        @pl.when(ok)
        def _(d=d):
            greet(near_id(d))

        count = count + jnp.where(ok, 1, 0)

    @pl.when(seg > 0)
    def _():
        greet((seg - 1, r, c))

    @pl.when(seg < SEGS - 1)
    def _():
        greet((seg + 1, r, c))

    count = count + jnp.where(seg > 0, 1, 0) + jnp.where(seg < SEGS - 1, 1, 0)

    sources = (saved_h, taps_h, cbias_h, gain_h, nbias_h, w_in_h, b_in_h, w_out_h, lscale_h, tissue_h, og_h)
    places = (saved, taps, cbias, gain, nbias, w_in, b_in, w_out, lscale, tissue, og)
    loads = [pltpu.make_async_copy(a, b, load_sem.at[n]) for n, (a, b) in enumerate(zip(sources, places))]
    for load in loads:
        load.start()

    def stage_cols(pad, p, row0):
        piece = slice(4 * row0, 4 * row0 + 16)
        for side, first in ((0, LEFT), (1, LEFT + W - 4)):
            for h in range(2):
                for q in range(row0, row0 + CONV_ROWS):
                    strip[side, 4 * q : 4 * q + 4, h * 128 : (h + 1) * 128] = pad[h, 3 + q, first : first + 4, :]
            col_s[p, side, piece] = strip[side, piece].astype(BF16)

    loads[0].wait()
    for h in range(2):
        xpad[h, 3 : 3 + H, LEFT : LEFT + W, :] = saved[:, :, h * 128 : (h + 1) * 128].astype(F32)
    for row0 in ORDER:
        stage_cols(xpad, 0, row0)

    def landing(p, d, m=0):
        if d < 2:
            return row_r.at[p, d]
        if d < 4:
            return col_r.at[p, d - 2, pl.ds(16 * m, 16)]
        return cor_r.at[p, d - 4]

    def slot(d, m=0):
        return d if d not in (2, 3) else 8 + 4 * (d - 2) + m

    for p in range(2):
        for d in range(8):

            @pl.when(jnp.logical_not(near_ok(d)))
            def _(p=p, d=d):
                for m in range(4 if d in (2, 3) else 1):
                    ref = landing(p, d, m)
                    ref[...] = jnp.zeros(ref.shape, BF16)

    pl.semaphore_wait(barrier, count)

    def halo_copy(p, tile, d, m=0):
        dr, dc = DIRS[d]
        side = 0 if dc < 0 else 1
        if dc == 0:
            src = tile.at[0:3] if dr < 0 else tile.at[H - 3 : H]
        elif dr == 0:
            src = col_s.at[p, side, pl.ds(16 * m, 16)]
        else:
            src = col_s.at[p, side, pl.ds(0 if dr < 0 else 4 * H - 16, 16)]
        return pltpu.make_async_remote_copy(
            src_ref=src,
            dst_ref=landing(p, BACK[d], m),
            send_sem=halo_send.at[p, slot(d, m)],
            recv_sem=halo_recv.at[p, slot(BACK[d], m)],
            device_id=near_id(d),
            device_id_type=MESH,
        )

    def messages(row0):
        m = row0 // CONV_ROWS
        edge = ((4, 0), (5, 0), (0, 0)) if row0 == 0 else ((6, 0), (7, 0), (1, 0)) if row0 == H - CONV_ROWS else ()
        return edge + ((2, m), (3, m))

    def halo_start(p, tile, row0):
        for d, m in messages(row0):

            @pl.when(near_ok(d))
            def _(d=d, m=m):
                halo_copy(p, tile, d, m).start()

    def halo_wait(p, row0):
        for d, m in messages(row0):

            @pl.when(near_ok(d))
            def _(d=d, m=m):
                pltpu.make_async_remote_copy(
                    src_ref=landing(p, d, m),
                    dst_ref=landing(p, d, m),
                    send_sem=halo_send.at[p, slot(d, m)],
                    recv_sem=halo_recv.at[p, slot(d, m)],
                    device_id=near_id(d),
                    device_id_type=MESH,
                ).wait_recv()

    def halo_drain(p, tile):
        for row0 in ORDER:
            for d, m in messages(row0):

                @pl.when(near_ok(d))
                def _(d=d, m=m):
                    halo_copy(p, tile, d, m).wait_send()

    def unpack(pad, p, row0):
        piece = slice(4 * row0, 4 * row0 + 16)
        for side, first in ((0, LEFT - 4), (1, LEFT + W)):
            strip[side, piece] = col_r[p, side, piece].astype(F32)
            for h in range(2):
                for q in range(row0, row0 + CONV_ROWS):
                    pad[h, 3 + q, first : first + 4, :] = strip[side, 4 * q : 4 * q + 4, h * 128 : (h + 1) * 128]
        if row0 not in (0, H - CONV_ROWS):
            return
        top = row0 == 0
        base, src0 = (0, 1) if top else (3 + H, 0)
        for side, first in ((0, LEFT - 4), (1, LEFT + W)):
            k = side + (0 if top else 2)
            corner[k] = cor_r[p, k].astype(F32)
            for h in range(2):
                for q in range(3):
                    m = 4 * (src0 + q)
                    pad[h, base + q, first : first + 4, :] = corner[k, m : m + 4, h * 128 : (h + 1) * 128]
        for h in range(2):
            lanes = slice(h * 128, (h + 1) * 128)
            pad[h, base : base + 3, LEFT : LEFT + W, :] = row_r[p, 0 if top else 1, :, :, lanes].astype(F32)

    for row0 in ORDER:
        halo_start(0, saved, row0)
    for load in loads[1:]:
        load.wait()
    for row0 in ORDER:
        halo_wait(0, row0)
        unpack(xpad, 0, row0)

    @pl.loop(0, H // CONV_ROWS)
    def _(n):
        conv = conv_rows(xpad, taps, n * CONV_ROWS, False) + cbias[...]
        pix = pl.ds(pl.multiple_of(n * (CONV_ROWS * W), CONV_ROWS * W), CONV_ROWS * W)
        centred = conv - jnp.mean(conv, axis=-1, keepdims=True)
        inv_std = lax.rsqrt(jnp.mean(centred * centred, axis=-1, keepdims=True) + EPS)
        standard = centred * inv_std
        std[pix, :] = standard
        inv[pix, :] = jnp.broadcast_to(inv_std, (CONV_ROWS * W, 128))
        nbuf[pix, :] = (standard * gain[...] + nbias[...]).astype(BF16)

    @pl.loop(0, HID // 256)
    def _(n):
        units = pl.ds(pl.multiple_of(n * 256, 256), 256)
        pre = jnp.dot(nbuf[...], w_in[:, units], preferred_element_type=F32) + b_in[:, units]
        square = pre * pre
        th = jnp.tanh(GELU_A * (pre + GELU_B * (square * pre)))
        half = 0.5 * (1.0 + th)
        hbuf[:, units] = (pre * half).astype(BF16)
        slope = GELU_A * (1.0 + (3.0 * GELU_B) * square)
        dgelu[:, units] = half + 0.5 * pre * (1.0 - th * th) * slope

    def shift_copy(src, n):
        rows = pl.ds(ORDER[n], CONV_ROWS)
        return pltpu.make_async_remote_copy(
            src_ref=src.at[rows],
            dst_ref=gin.at[rows],
            send_sem=shift_send.at[n],
            recv_sem=shift_recv.at[n],
            device_id=(lax.rem(seg + SEGS - 1, SEGS), r, c),
            device_id_type=MESH,
        )

    mask = tissue[...].astype(F32)

    def turn():
        tbuf[...] = nbuf[...].T
        for n in range(HID // 256):
            htbuf[n * 256 : (n + 1) * 256, :] = hbuf[:, n * 256 : (n + 1) * 256].T

    @pl.when(seg == SEGS - 1)
    def _():
        gin[...] = og[...]

    @pl.when(seg < SEGS - 1)
    def _():
        turn()

    for n, row0 in enumerate(ORDER):

        @pl.when(seg < SEGS - 1)
        def _(n=n):
            shift_copy(out, n).wait_recv()

        rows = slice(row0, row0 + CONV_ROWS)
        pix = slice(row0 * W, row0 * W + CH_PIX)
        upstream = gin[rows].reshape(CH_PIX, C).astype(F32)
        bg = (mask * lscale[...] * upstream).astype(BF16)
        bgb[pix, :] = bg
        hidden_grad = lax.dot_general(bg, w_out[...], NT, preferred_element_type=F32)
        pg = (hidden_grad * dgelu[pix, :]).astype(BF16)
        pgb[pix, :] = pg
        ng = lax.dot_general(pg, w_in[...], NT, preferred_element_type=F32) * gain[...]
        standard = std[pix, :]
        m1 = jnp.mean(ng, axis=-1, keepdims=True)
        m2 = jnp.mean(ng * standard, axis=-1, keepdims=True)
        cg = (inv[pix, 0:1] * (ng - m1 - standard * m2)).astype(BF16)
        cgt[rows] = cg.reshape(CONV_ROWS, W, C)
        wide = cg.astype(F32).reshape(CONV_ROWS, W, C)
        for h in range(2):
            gpad[h, 3 + row0 : 3 + row0 + CONV_ROWS, LEFT : LEFT + W, :] = wide[:, :, h * 128 : (h + 1) * 128]
        stage_cols(gpad, 1, row0)
        halo_start(1, cgt, row0)

    def remote(src, dst, send, recv, device):
        return pltpu.make_async_remote_copy(
            src_ref=src, dst_ref=dst, send_sem=send, recv_sem=recv,
            device_id=device, device_id_type=MESH,
        )

    def all_of(ref, send, recv):
        return remote(ref, ref, send, recv, sib)

    def sib_copy(src, dst, k):
        return remote(src, dst, sib_send.at[k], sib_recv.at[k], sib)

    other = 1 - core
    first_i = sib_copy(s0i.at[other], r0i, 0)
    first_o = sib_copy(s0o.at[other], r0o, 1)
    tap_a = sib_copy(ts0.at[other], tr0, 2)

    def gradients():
        for n in range(HID // 256):
            units = slice(n * 256, (n + 1) * 256)
            gi = jnp.dot(tbuf[...], pgb[:, units], preferred_element_type=F32) * scale
            gi = gi.astype(BF16)
            for k in range(COLS):
                s0i[k % 2, k // 2, :, units] = gi[16 * k : 16 * k + 16]
        first_i.start()
        for n in range(HID // 256):
            go = jnp.dot(htbuf[n * 256 : (n + 1) * 256, :], bgb[...], preferred_element_type=F32) * scale
            go = go.astype(BF16)
            for k in range(4):
                owner = n * 4 + k
                s0o[owner % 2, owner // 2] = go[64 * k : 64 * k + 64]
        first_o.start()
        for h in range(2):
            for j in range(7):
                sums = [jnp.zeros((8, 128), F32) for _ in range(7)]
                for block in range(H // CONV_ROWS):
                    row0 = block * CONV_ROWS
                    window = xpad[h, row0 : row0 + CONV_ROWS + 6, LEFT - 3 + j : LEFT - 3 + j + W, :]
                    grad = gpad[h, 3 + row0 : 3 + row0 + CONV_ROWS, LEFT : LEFT + W, :]
                    for i in range(7):
                        prod = (window[i : i + CONV_ROWS] * grad).reshape(2 * CONV_ROWS, 8, 128)
                        sums[i] = sums[i] + jnp.sum(prod, axis=0)
                for i in range(7):
                    tacc[h, 7 * i + j] = sums[i]
        for h in range(2):
            ts0[h] = jnp.zeros((64, 128), BF16)
            ts0[h, 0:49] = (jnp.sum(tacc[h], axis=1) * scale).astype(BF16)
        tap_a.start()

    @pl.when(seg == 0)
    def _():
        gradients()

    for n, row0 in enumerate(ORDER):
        for needed in ((0, 4), (12, 8))[n] if n < 2 else ():
            halo_wait(1, needed)
            unpack(gpad, 1, needed)
        total = conv_rows(gpad, taps, row0, True).reshape(CONV_ROWS, W, C)
        total = gin[row0 : row0 + CONV_ROWS].astype(F32) + total
        out[row0 : row0 + CONV_ROWS] = total.astype(BF16)

        @pl.when(seg > 0)
        def _(n=n):
            shift_copy(out, n).start()

    @pl.when(seg == SEGS - 1)
    def _():
        turn()

    @pl.when(seg > 0)
    def _():
        gradients()

    first_i.wait()
    for k in range(YS):
        t1i[k] = (s0i[core, k].astype(F32) + r0i[k].astype(F32)).astype(BF16)

    def a_copy(k):
        p = ypeer(k)
        return remote(t1i.at[p], r1i.at[k - 1], a_send, a_recv, (seg, r, 2 * p + core))

    for k in FAR:
        a_copy(k).start()
    first_o.wait()
    for k in range(YS):
        both = s0o[core, k].astype(F32) + r0o[k].astype(F32)
        both = both.astype(BF16)
        for q in range(ROWS):
            t1o[q, k] = both[16 * (q // 2) : 16 * (q // 2) + 16, 128 * (q % 2) : 128 * (q % 2) + 128]

    def b_copy(k):
        p = zpeer(k)
        return remote(t1o.at[p], r1o.at[k - 1], b_send, b_recv, (seg, p, c))

    for k in FAR:
        b_copy(k).start()

    tap_a.wait()
    try_[y] = (ts0[core].astype(F32) + tr0[...].astype(F32)).astype(BF16)

    def ty_copy(k):
        return remote(try_.at[y], try_.at[y], ty_send, ty_recv, (seg, r, 2 * ypeer(k) + core))

    for k in FAR:
        ty_copy(k).start()

    all_of(r1i, a_send, a_recv).wait_recv()
    mine = t1i[y].astype(F32)
    for k in range(7):
        mine = mine + r1i[k].astype(F32)
    mine = mine.astype(BF16)
    for q in range(ROWS):
        p2i[q] = mine[:, 128 * q : 128 * q + 128]

    def c_copy(k):
        p = zpeer(k)
        return remote(p2i.at[p], r2i.at[k - 1], c_send, c_recv, (seg, p, c))

    for k in FAR:
        c_copy(k).start()

    all_of(r1o, b_send, b_recv).wait_recv()
    part = t1o[r].astype(F32)
    for k in range(7):
        part = part + r1o[k].astype(F32)
    p2o[...] = part.astype(BF16)

    def d_copy(k):
        p = ypeer(k)
        return remote(p2o.at[p], r2o.at[k - 1], d_send, d_recv, (seg, r, 2 * p + core))

    for k in FAR:
        d_copy(k).start()

    all_of(try_.at[pl.ds(0, 7)], ty_send, ty_recv).wait_recv()
    tsum = try_[0].astype(F32)
    for k in range(1, 8):
        tsum = tsum + try_[k].astype(F32)
    trz[r] = tsum.astype(BF16)

    def tz_copy(k):
        return remote(trz.at[r], trz.at[r], tz_send, tz_recv, (seg, zpeer(k), c))

    for k in FAR:
        tz_copy(k).start()

    all_of(r2i, c_send, c_recv).wait_recv()
    full_i = p2i[r].astype(F32)
    for k in range(7):
        full_i = full_i + r2i[k].astype(F32)
    all_of(r2o, d_send, d_recv).wait_recv()
    full_o = p2o[y].astype(F32)
    for k in range(7):
        full_o = full_o + r2o[k].astype(F32)
    r3[r, 0] = full_i
    r3[r, 1] = full_o

    def e_copy(k):
        return remote(r3.at[r], r3.at[r], e_send, e_recv, (seg, zpeer(k), c))

    for k in FAR:
        e_copy(k).start()

    all_of(trz.at[pl.ds(0, 7)], tz_send, tz_recv).wait_recv()
    tsum = trz[0].astype(F32)
    for k in range(1, 8):
        tsum = tsum + trz[k].astype(F32)
    tfin[core] = tsum
    tap_b = sib_copy(tfin.at[core], tfin.at[core], 3)
    tap_b.start()

    all_of(r3.at[pl.ds(0, 7)], e_send, e_recv).wait_recv()
    for q in range(ROWS):
        gi_out[:, 128 * q : 128 * q + 128] = r3[q, 0]
        go_out[16 * (q // 2) : 16 * (q // 2) + 16, 128 * (q % 2) : 128 * (q % 2) + 128] = r3[q, 1]

    tap_b.wait_send()
    sib_copy(tfin.at[other], tfin.at[other], 3).wait_recv()
    for h in range(2):
        for i in range(7):
            taps_out[i, :, 0, h * 128 : (h + 1) * 128] = tfin[h, 7 * i : 7 * i + 7, :]

    halo_drain(0, saved)
    halo_drain(1, cgt)
    for n in range(CHUNKS):

        @pl.when(seg > 0)
        def _(n=n):
            shift_copy(out, n).wait_send()

    for ref, send, recv in (
        (r1i, a_send, a_recv),
        (r1o, b_send, b_recv),
        (r2i, c_send, c_recv),
        (r2o, d_send, d_recv),
        (r3.at[pl.ds(0, 7)], e_send, e_recv),
        (try_.at[pl.ds(0, 7)], ty_send, ty_recv),
        (trz.at[pl.ds(0, 7)], tz_send, tz_recv),
    ):
        all_of(ref, send, recv).wait_send()


def place(a, b, c, d, a_out, b_out, c_out, d_out, sem):
    pairs = zip((a, b, c, d), (a_out, b_out, c_out, d_out))
    copies = [pltpu.make_async_copy(x, z, sem.at[n]) for n, (x, z) in enumerate(pairs)]
    for copy in copies:
        copy.start()
    for copy in copies:
        copy.wait()


def per_device(
    saved_inputs, out_grad, tissue, conv_taps, conv_bias, norm_gain, norm_bias,
    w_in, b_in, w_out, layer_scale,
):
    scale = 1.0 / math.sqrt(ROWS * H * COLS * W)
    vmem = pl.BlockSpec(memory_space=pltpu.VMEM)
    dma = pltpu.SemaphoreType.DMA
    px = H * W
    out, gi, go, gt = pl.pallas_call(
        functools.partial(body, scale),
        out_shape=(
            pltpu.VMEM((H, W, C), BF16),
            pltpu.VMEM((C // COLS, HID), F32),
            pltpu.VMEM((HID // COLS, C), F32),
            pltpu.VMEM((7, 7, 1, C), F32),
        ),
        in_specs=[pl.BlockSpec(memory_space=pl.ANY)] * 11,
        out_specs=(vmem, vmem, vmem, vmem),
        scratch_shapes=[
            pltpu.VMEM((H, W, C), BF16),
            pltpu.VMEM((H, W, C), BF16),
            pltpu.VMEM((1, 1), jnp.int32),
            pltpu.VMEM((7, 7, 1, C), F32),
            pltpu.VMEM((1, C), F32),
            pltpu.VMEM((1, C), F32),
            pltpu.VMEM((1, C), F32),
            pltpu.VMEM((C, HID), BF16),
            pltpu.VMEM((1, HID), F32),
            pltpu.VMEM((HID, C), BF16),
            pltpu.VMEM((1, C), F32),
            dma((11,)),
            pltpu.VMEM((C, px), BF16),
            pltpu.VMEM((HID, px), BF16),
            pltpu.VMEM((2, H + 6, PADW, 128), F32),
            pltpu.VMEM((2, H + 6, PADW, 128), F32),
            pltpu.VMEM((px, C), F32),
            pltpu.VMEM((px, 128), F32),
            pltpu.VMEM((px, C), BF16),
            pltpu.VMEM((px, HID), BF16),
            pltpu.VMEM((px, HID), F32),
            pltpu.VMEM((px, C), BF16),
            pltpu.VMEM((px, HID), BF16),
            pltpu.VMEM((H, W, C), BF16),
            pltpu.VMEM((H, W, C), BF16),
            pltpu.VMEM((2, 2, 4 * H, C), BF16),
            pltpu.VMEM((2, 2, 3, W, C), BF16),
            pltpu.VMEM((2, 2, 4 * H, C), BF16),
            pltpu.VMEM((2, 4, 16, C), BF16),
            pltpu.VMEM((2, 4 * H, C), F32),
            pltpu.VMEM((4, 16, C), F32),
            pltpu.VMEM((2, YS, 16, HID), BF16),
            pltpu.VMEM((2, YS, 64, C), BF16),
            pltpu.VMEM((YS, 16, HID), BF16),
            pltpu.VMEM((YS, 64, C), BF16),
            pltpu.VMEM((YS, 16, HID), BF16),
            pltpu.VMEM((ROWS, YS, 16, 128), BF16),
            pltpu.VMEM((7, 16, HID), BF16),
            pltpu.VMEM((7, YS, 16, 128), BF16),
            pltpu.VMEM((ROWS, 16, 128), BF16),
            pltpu.VMEM((YS, 16, 128), BF16),
            pltpu.VMEM((7, 16, 128), BF16),
            pltpu.VMEM((7, 16, 128), BF16),
            pltpu.VMEM((ROWS, 2, 16, 128), F32),
            pltpu.VMEM((2, 49, 8, 128), F32),
            pltpu.VMEM((2, 64, 128), BF16),
            pltpu.VMEM((64, 128), BF16),
            pltpu.VMEM((YS, 64, 128), BF16),
            pltpu.VMEM((ROWS, 64, 128), BF16),
            pltpu.VMEM((2, 64, 128), F32),
            dma((2, 16)), dma((2, 16)), dma((CHUNKS,)), dma((CHUNKS,)),
            dma((4,)), dma((4,)),
            dma, dma, dma, dma, dma, dma, dma, dma,
            dma, dma, dma, dma, dma, dma,
        ],
        compiler_params=pltpu.CompilerParams(collective_id=0, has_side_effects=True),
    )(*(operand for operand in (
        saved_inputs[0, 0], out_grad[0], tissue[0], conv_taps.reshape(7, 7, 1, C), conv_bias, norm_gain, norm_bias,
        w_in[0], b_in, w_out[0], layer_scale,
    )))
    results = (out, gi, go, gt)
    hbm = pl.BlockSpec(memory_space=pl.ANY)
    out, gi, go, gt = pl.pallas_call(
        place,
        out_shape=tuple(jax.ShapeDtypeStruct(a.shape, a.dtype) for a in results),
        in_specs=[vmem] * 4,
        out_specs=(hbm, hbm, hbm, hbm),
        scratch_shapes=[dma((4,))],
        compiler_params=pltpu.CompilerParams(vmem_limit_bytes=4 * 1024 * 1024),
    )(*results)
    return (out[None, None], gi[None], go[None], gt.reshape(1, 7, 7, C))


def solution(mesh):
    return jax.shard_map(
        per_device,
        mesh=mesh,
        in_specs=(
            P("segment", None, "row", "col", None),
            P(None, "row", "col", None),
            P(None, "row", "col"),
            P("segment", None, None, None),
            P("segment", None),
            P("segment", None),
            P("segment", None),
            P("segment", None, None),
            P("segment", None),
            P("segment", None, None),
            P("segment", None),
        ),
        out_specs=(
            P("segment", None, "row", "col", None),
            P("segment", "col", None),
            P("segment", "col", None),
            P("segment", None, None, None),
        ),
        check_vma=False,
    )
```

time: 90.3 us -> 73.5 us (0.81)
  Pallas kernels: 82.7 us -> 72.1 us
  local copies, waits for them, and re-layouts: 6.02 us -> 0 us
    pallas_call x1 -> x2, Pallas kernels: 82.7 us -> 72.1 us  [the longest x1 71.4 us: per_device(): pl.pallas_call(functools.partial(body, scale), out_shape=(pltpu.VMEM((H,...]
    unnamed x9 -> x0, local copies, waits for them, and re-layouts: 6.02 us -> none
where the time goes in v2:
time: 73.5 us; the launch traced here: 73.4 us
  Pallas kernels  72.1 us (98%)
  between operations  1.29 us (2%)
    pallas_call x1, Pallas kernels, per_device(): pl.pallas_call(functools.partial(body, scale), out_shape=(pltpu.VMEM((H,...  71.4 us

profile of v2, /device:TPU:1, one launch (start us, length us, event | category | flops | bytes accessed | tf_op | source)
XLA Modules:
  0.0 73.4 jit_solution(11175321331648271088)
XLA Ops:
  1.3 71.4 %shard_map.138 = (bf16[16,16,256]{2,1,0:T(8,128)(2,1)S(1)}, f32[16,1024]{1,0:T(8,128)S(1)}, f32[64,256]{1,0:T(8,128)S(1)}, f32[7,7,1,256]{3,2,1,0:T(1,128)S(1)}) custom-call(bf16[16,16,256]{2,1,0:T(8,128)(2,1)} %bitcast.13, bf16[16,16,256]{2,1,0:T(8,128)(2,1)} %bitcast.14, s32[1,1]{1,0:T(1,128)} %bitcast.10.tissue_h, f32[7,7,1,256]{3,2,1,0:T(1,128)} %bitcast.15, ...), custom_call_target="tpu_custom_call" | custom-call | tf_op jit(solution)/shard_map/pallas_call | solution.py:546
  72.7 0.7 %shard_map.139 = (bf16[16,16,256]{2,1,0:T(8,128)(2,1)}, f32[16,1024]{1,0:T(8,128)}, f32[64,256]{1,0:T(8,128)}, f32[7,7,1,256]{3,2,1,0:T(1,128)}) custom-call(bf16[16,16,256]{2,1,0:T(8,128)(2,1)S(1)} %get-tuple-element.12.a, f32[16,1024]{1,0:T(8,128)S(1)} %get-tuple-element.13.b, f32[64,256]{1,0:T(8,128)S(1)} %get-tuple-element.14.c, ...), custom_call_target="tpu_custom_call" | custom-call | tf_op jit(solution)/shard_map/pallas_call | solution.py:619

commit v3 on v2

--- a/solution.py
+++ b/solution.py
@@ -32,8 +32,6 @@
 FAR = (4, 3, 5, 2, 6, 1, 7)
 GELU_A = math.sqrt(2.0 / math.pi)
 GELU_B = 0.044715
-NT = (((1,), (1,)), ((), ()))
-TN = (((0,), (0,)), ((), ()))
 
 
 def conv_rows(pad, taps, row0, flip):
@@ -54,7 +52,7 @@
     scale,
     saved_h, og_h, tissue_h, taps_h, cbias_h, gain_h, nbias_h, w_in_h, b_in_h, w_out_h, lscale_h,
     out, gi_out, go_out, taps_out,
-    saved, og, tissue, taps, cbias, gain, nbias, w_in, b_in, w_out, lscale, load_sem, tbuf, htbuf,
+    saved, og, tissue, taps, cbias, gain, nbias, w_in, b_in, w_out, lscale, load_sem, tbuf, htbuf, wo_t, wi_t,
     xpad, gpad, std, inv, nbuf, hbuf, dgelu, bgb, pgb, gin, cgt,
     col_s, row_r, col_r, cor_r, strip, corner,
     s0i, s0o, r0i, r0o, t1i, t1o, r1i, r1o, p2i, p2o, r2i, r2o, r3,
@@ -92,6 +90,12 @@
     def ypeer(k):
         return lax.rem(y + k, YS)
 
+    sources = (saved_h, taps_h, cbias_h, gain_h, nbias_h, w_in_h, b_in_h, w_out_h, lscale_h, tissue_h, og_h)
+    places = (saved, taps, cbias, gain, nbias, w_in, b_in, w_out, lscale, tissue, og)
+    loads = [pltpu.make_async_copy(a, b, load_sem.at[n]) for n, (a, b) in enumerate(zip(sources, places))]
+    for load in loads:
+        load.start()
+
     barrier = pltpu.get_barrier_semaphore()
 
     def greet(device):
@@ -126,12 +130,6 @@
         greet((seg + 1, r, c))
 
     count = count + jnp.where(seg > 0, 1, 0) + jnp.where(seg < SEGS - 1, 1, 0)
-
-    sources = (saved_h, taps_h, cbias_h, gain_h, nbias_h, w_in_h, b_in_h, w_out_h, lscale_h, tissue_h, og_h)
-    places = (saved, taps, cbias, gain, nbias, w_in, b_in, w_out, lscale, tissue, og)
-    loads = [pltpu.make_async_copy(a, b, load_sem.at[n]) for n, (a, b) in enumerate(zip(sources, places))]
-    for load in loads:
-        load.start()
 
     def stage_cols(pad, p, row0):
         piece = slice(4 * row0, 4 * row0 + 16)
@@ -246,6 +244,10 @@
         halo_start(0, saved, row0)
     for load in loads[1:]:
         load.wait()
+    for n in range(HID // 256):
+        units = slice(n * 256, (n + 1) * 256)
+        wo_t[:, units] = w_out[units, :].T
+        wi_t[units, :] = w_in[:, units].T
     for row0 in ORDER:
         halo_wait(0, row0)
         unpack(xpad, 0, row0)
@@ -309,10 +311,10 @@
         upstream = gin[rows].reshape(CH_PIX, C).astype(F32)
         bg = (mask * lscale[...] * upstream).astype(BF16)
         bgb[pix, :] = bg
-        hidden_grad = lax.dot_general(bg, w_out[...], NT, preferred_element_type=F32)
+        hidden_grad = jnp.dot(bg, wo_t[...], preferred_element_type=F32)
         pg = (hidden_grad * dgelu[pix, :]).astype(BF16)
         pgb[pix, :] = pg
-        ng = lax.dot_general(pg, w_in[...], NT, preferred_element_type=F32) * gain[...]
+        ng = jnp.dot(pg, wi_t[...], preferred_element_type=F32) * gain[...]
         standard = std[pix, :]
         m1 = jnp.mean(ng, axis=-1, keepdims=True)
         m2 = jnp.mean(ng * standard, axis=-1, keepdims=True)
@@ -373,62 +375,78 @@
             ts0[h, 0:49] = (jnp.sum(tacc[h], axis=1) * scale).astype(BF16)
         tap_a.start()
 
-    @pl.when(seg == 0)
-    def _():
-        gradients()
-
-    for n, row0 in enumerate(ORDER):
-        for needed in ((0, 4), (12, 8))[n] if n < 2 else ():
-            halo_wait(1, needed)
-            unpack(gpad, 1, needed)
-        total = conv_rows(gpad, taps, row0, True).reshape(CONV_ROWS, W, C)
-        total = gin[row0 : row0 + CONV_ROWS].astype(F32) + total
-        out[row0 : row0 + CONV_ROWS] = total.astype(BF16)
-
-        @pl.when(seg > 0)
-        def _(n=n):
-            shift_copy(out, n).start()
-
-    @pl.when(seg == SEGS - 1)
-    def _():
-        turn()
-
-    @pl.when(seg > 0)
-    def _():
-        gradients()
-
-    first_i.wait()
-    for k in range(YS):
-        t1i[k] = (s0i[core, k].astype(F32) + r0i[k].astype(F32)).astype(BF16)
+    near = jnp.where(core == 0, y, r)
+    away = jnp.where(core == 0, r, y)
+
+    def side_peer(k, along_y):
+        return (seg, jnp.where(along_y, r, zpeer(k)), jnp.where(along_y, 2 * ypeer(k) + core, c))
 
     def a_copy(k):
         p = ypeer(k)
         return remote(t1i.at[p], r1i.at[k - 1], a_send, a_recv, (seg, r, 2 * p + core))
 
-    for k in FAR:
-        a_copy(k).start()
-    first_o.wait()
-    for k in range(YS):
-        both = s0o[core, k].astype(F32) + r0o[k].astype(F32)
-        both = both.astype(BF16)
-        for q in range(ROWS):
-            t1o[q, k] = both[16 * (q // 2) : 16 * (q // 2) + 16, 128 * (q % 2) : 128 * (q % 2) + 128]
-
     def b_copy(k):
         p = zpeer(k)
         return remote(t1o.at[p], r1o.at[k - 1], b_send, b_recv, (seg, p, c))
 
-    for k in FAR:
-        b_copy(k).start()
-
-    tap_a.wait()
-    try_[y] = (ts0[core].astype(F32) + tr0[...].astype(F32)).astype(BF16)
-
     def ty_copy(k):
-        return remote(try_.at[y], try_.at[y], ty_send, ty_recv, (seg, r, 2 * ypeer(k) + core))
-
-    for k in FAR:
-        ty_copy(k).start()
+        return remote(try_.at[near], try_.at[near], ty_send, ty_recv, side_peer(k, core == 0))
+
+    def input_gradient():
+        for n, row0 in enumerate(ORDER):
+            for needed in ((0, 4), (12, 8))[n] if n < 2 else ():
+                halo_wait(1, needed)
+                unpack(gpad, 1, needed)
+            total = conv_rows(gpad, taps, row0, True).reshape(CONV_ROWS, W, C)
+            total = gin[row0 : row0 + CONV_ROWS].astype(F32) + total
+            out[row0 : row0 + CONV_ROWS] = total.astype(BF16)
+
+            @pl.when(seg > 0)
+            def _(n=n):
+                shift_copy(out, n).start()
+
+    def first_stage():
+        first_i.wait()
+        for k in range(YS):
+            t1i[k] = (s0i[core, k].astype(F32) + r0i[k].astype(F32)).astype(BF16)
+
+        for k in FAR:
+            a_copy(k).start()
+        first_o.wait()
+        for k in range(YS):
+            both = s0o[core, k].astype(F32) + r0o[k].astype(F32)
+            both = both.astype(BF16)
+            for q in range(ROWS):
+                t1o[q, k] = both[16 * (q // 2) : 16 * (q // 2) + 16, 128 * (q % 2) : 128 * (q % 2) + 128]
+
+        for k in FAR:
+            b_copy(k).start()
+
+        tap_a.wait()
+        try_[near] = (ts0[core].astype(F32) + tr0[...].astype(F32)).astype(BF16)
+
+        for k in FAR:
+            ty_copy(k).start()
+
+    @pl.when(seg == 0)
+    def _():
+        gradients()
+        first_stage()
+        input_gradient()
+
+    @pl.when(seg == SEGS - 1)
+    def _():
+        input_gradient()
+        turn()
+
+    @pl.when(jnp.logical_and(seg > 0, seg < SEGS - 1))
+    def _():
+        input_gradient()
+
+    @pl.when(seg > 0)
+    def _():
+        gradients()
+        first_stage()
 
     all_of(r1i, a_send, a_recv).wait_recv()
     mine = t1i[y].astype(F32)
@@ -462,10 +480,10 @@
     tsum = try_[0].astype(F32)
     for k in range(1, 8):
         tsum = tsum + try_[k].astype(F32)
-    trz[r] = tsum.astype(BF16)
+    trz[away] = tsum.astype(BF16)
 
     def tz_copy(k):
-        return remote(trz.at[r], trz.at[r], tz_send, tz_recv, (seg, zpeer(k), c))
+        return remote(trz.at[away], trz.at[away], tz_send, tz_recv, side_peer(k, core == 1))
 
     for k in FAR:
         tz_copy(k).start()
@@ -478,8 +496,8 @@
     full_o = p2o[y].astype(F32)
     for k in range(7):
         full_o = full_o + r2o[k].astype(F32)
-    r3[r, 0] = full_i
-    r3[r, 1] = full_o
+    r3[r, 0] = full_i.astype(BF16)
+    r3[r, 1] = full_o.astype(BF16)
 
     def e_copy(k):
         return remote(r3.at[r], r3.at[r], e_send, e_recv, (seg, zpeer(k), c))
@@ -497,8 +515,8 @@
 
     all_of(r3.at[pl.ds(0, 7)], e_send, e_recv).wait_recv()
     for q in range(ROWS):
-        gi_out[:, 128 * q : 128 * q + 128] = r3[q, 0]
-        go_out[16 * (q // 2) : 16 * (q // 2) + 16, 128 * (q % 2) : 128 * (q % 2) + 128] = r3[q, 1]
+        gi_out[:, 128 * q : 128 * q + 128] = r3[q, 0].astype(F32)
+        go_out[16 * (q // 2) : 16 * (q // 2) + 16, 128 * (q % 2) : 128 * (q % 2) + 128] = r3[q, 1].astype(F32)
 
     tap_b.wait_send()
     sib_copy(tfin.at[other], tfin.at[other], 3).wait_recv()
@@ -568,6 +586,8 @@
             dma((11,)),
             pltpu.VMEM((C, px), BF16),
             pltpu.VMEM((HID, px), BF16),
+            pltpu.VMEM((C, HID), BF16),
+            pltpu.VMEM((HID, C), BF16),
             pltpu.VMEM((2, H + 6, PADW, 128), F32),
             pltpu.VMEM((2, H + 6, PADW, 128), F32),
             pltpu.VMEM((px, C), F32),
@@ -597,7 +617,7 @@
             pltpu.VMEM((YS, 16, 128), BF16),
             pltpu.VMEM((7, 16, 128), BF16),
             pltpu.VMEM((7, 16, 128), BF16),
-            pltpu.VMEM((ROWS, 2, 16, 128), F32),
+            pltpu.VMEM((ROWS, 2, 16, 128), BF16),
             pltpu.VMEM((2, 49, 8, 128), F32),
             pltpu.VMEM((2, 64, 128), BF16),
             pltpu.VMEM((64, 128), BF16),

time: 73.5 us -> 70.3 us (0.956)
  Pallas kernels: 72.1 us -> 68.6 us
    pallas_call x1, Pallas kernels: 71.4 us -> 67.8 us  [per_device(): pl.pallas_call(functools.partial(body, scale), out_shape=(pltpu.VMEM((H,...]
where the time goes in v3:
time: 70.3 us; the launch traced here: 69.9 us
  Pallas kernels  68.6 us (98%)
  between operations  1.29 us (2%)
    pallas_call x1, Pallas kernels, per_device(): pl.pallas_call(functools.partial(body, scale), out_shape=(pltpu.VMEM((H,...  67.8 us

profile of v3, /device:TPU:1, one launch (start us, length us, event | category | flops | bytes accessed | tf_op | source)
XLA Modules:
  0.0 69.9 jit_solution(7620116234712484749)
XLA Ops:
  1.3 67.8 %shard_map.138 = (bf16[16,16,256]{2,1,0:T(8,128)(2,1)S(1)}, f32[16,1024]{1,0:T(8,128)S(1)}, f32[64,256]{1,0:T(8,128)S(1)}, f32[7,7,1,256]{3,2,1,0:T(1,128)S(1)}) custom-call(bf16[16,16,256]{2,1,0:T(8,128)(2,1)} %bitcast.13, bf16[16,16,256]{2,1,0:T(8,128)(2,1)} %bitcast.14, s32[1,1]{1,0:T(1,128)} %bitcast.10.tissue_h, f32[7,7,1,256]{3,2,1,0:T(1,128)} %bitcast.15, ...), custom_call_target="tpu_custom_call" | custom-call | tf_op jit(solution)/shard_map/pallas_call | solution.py:564
  69.1 0.7 %shard_map.139 = (bf16[16,16,256]{2,1,0:T(8,128)(2,1)}, f32[16,1024]{1,0:T(8,128)}, f32[64,256]{1,0:T(8,128)}, f32[7,7,1,256]{3,2,1,0:T(1,128)}) custom-call(bf16[16,16,256]{2,1,0:T(8,128)(2,1)S(1)} %get-tuple-element.12.a, f32[16,1024]{1,0:T(8,128)S(1)} %get-tuple-element.13.b, f32[64,256]{1,0:T(8,128)S(1)} %get-tuple-element.14.c, ...), custom_call_target="tpu_custom_call" | custom-call | tf_op jit(solution)/shard_map/pallas_call | solution.py:639

commit v4 on v3

--- a/solution.py
+++ b/solution.py
@@ -252,10 +252,9 @@
         halo_wait(0, row0)
         unpack(xpad, 0, row0)
 
-    @pl.loop(0, H // CONV_ROWS)
-    def _(n):
-        conv = conv_rows(xpad, taps, n * CONV_ROWS, False) + cbias[...]
-        pix = pl.ds(pl.multiple_of(n * (CONV_ROWS * W), CONV_ROWS * W), CONV_ROWS * W)
+    for row0 in range(0, H, CONV_ROWS):
+        conv = conv_rows(xpad, taps, row0, False) + cbias[...]
+        pix = slice(row0 * W, (row0 + CONV_ROWS) * W)
         centred = conv - jnp.mean(conv, axis=-1, keepdims=True)
         inv_std = lax.rsqrt(jnp.mean(centred * centred, axis=-1, keepdims=True) + EPS)
         standard = centred * inv_std

time: 70.3 us -> 69.4 us (0.987)
  Pallas kernels: 68.6 us -> 67.6 us
    pallas_call x1, Pallas kernels: 67.8 us -> 66.9 us  [per_device(): pl.pallas_call(functools.partial(body, scale), out_shape=(pltpu.VMEM((H,...]
where the time goes in v4:
time: 69.4 us; the launch traced here: 68.9 us
  Pallas kernels  67.6 us (97%)
  between operations  1.29 us (2%)
    pallas_call x1, Pallas kernels, per_device(): pl.pallas_call(functools.partial(body, scale), out_shape=(pltpu.VMEM((H,...  66.9 us

profile of v4, /device:TPU:1, one launch (start us, length us, event | category | flops | bytes accessed | tf_op | source)
XLA Modules:
  0.0 68.9 jit_solution(14544451747640804737)
XLA Ops:
  1.3 66.9 %shard_map.138 = (bf16[16,16,256]{2,1,0:T(8,128)(2,1)S(1)}, f32[16,1024]{1,0:T(8,128)S(1)}, f32[64,256]{1,0:T(8,128)S(1)}, f32[7,7,1,256]{3,2,1,0:T(1,128)S(1)}) custom-call(bf16[16,16,256]{2,1,0:T(8,128)(2,1)} %bitcast.13, bf16[16,16,256]{2,1,0:T(8,128)(2,1)} %bitcast.14, s32[1,1]{1,0:T(1,128)} %bitcast.10.tissue_h, f32[7,7,1,256]{3,2,1,0:T(1,128)} %bitcast.15, ...), custom_call_target="tpu_custom_call" | custom-call | tf_op jit(solution)/shard_map/pallas_call | solution.py:563
  68.2 0.7 %shard_map.139 = (bf16[16,16,256]{2,1,0:T(8,128)(2,1)}, f32[16,1024]{1,0:T(8,128)}, f32[64,256]{1,0:T(8,128)}, f32[7,7,1,256]{3,2,1,0:T(1,128)}) custom-call(bf16[16,16,256]{2,1,0:T(8,128)(2,1)S(1)} %get-tuple-element.12.a, f32[16,1024]{1,0:T(8,128)S(1)} %get-tuple-element.13.b, f32[64,256]{1,0:T(8,128)S(1)} %get-tuple-element.14.c, ...), custom_call_target="tpu_custom_call" | custom-call | tf_op jit(solution)/shard_map/pallas_call | solution.py:638
